TPU v7x, 128 devices: a whole 4x4x4 slice. The times are simulated.
128 devices in a mesh: shard: 16 (over y, z), tensor: 8 (over x, core).
Axes of the slice: x: 4, y: 4, z: 4, core: 2. Of those that a mesh axis runs over, the one named last changes fastest.
Arguments:
- grads: bfloat16 [32, 896, 16640], P('shard', None, 'tensor'), may hold values from -1 to 1
- small_grads: bfloat16 [32, 2944], P('shard', 'tensor'), may hold values from -6 to 6
- counts: int32 [16], P('shard'), may hold values from 1 to 2
- step: int32 [1], replicated, may hold values from 1 to 1000
- master: float32 [896, 16640], P(('shard', 'tensor')), may hold values from -0.01953125 to 0.01953125
- moment_one: float32 [896, 16640], P(('shard', 'tensor')), may hold values from -7.6293945e-05 to 7.6293945e-05
- moment_two: float32 [896, 16640], P(('shard', 'tensor')), may hold values from 1e-12 to 1e-09
- average: float32 [896, 16640], P(('shard', 'tensor')), may hold values from -0.01953125 to 0.01953125
- small_master: float32 [8, 368], P('tensor', 'shard'), may hold values from -0.046875 to 0.046875
- small_one: float32 [8, 368], P('tensor', 'shard'), may hold values from -0.0078125 to 0.0078125
- small_two: float32 [8, 368], P('tensor', 'shard'), may hold values from 1e-09 to 1e-07
- small_average: float32 [8, 368], P('tensor', 'shard'), may hold values from -0.046875 to 0.046875
Outputs:
- new_master: float32 [896, 16640], P(('shard', 'tensor'))
- new_one: float32 [896, 16640], P(('shard', 'tensor'))
- new_two: float32 [896, 16640], P(('shard', 'tensor'))
- small_new: float32 [8, 368], P('tensor', 'shard')
- small_new_one: float32 [8, 368], P('tensor', 'shard')
- small_new_two: float32 [8, 368], P('tensor', 'shard')
- weights_out: bfloat16 [896, 16640], P(None, 'tensor')
- small_weights_out: bfloat16 [2944], P('tensor')
- average_out: float32 [896, 16640], P(None, 'tensor')
- small_average_out: float32 [2944], P('tensor')
All inputs are finite; a program needn't handle non-finite values.
Results may differ from a plain program's by a relative error of at most 0.001.
Values may be sent and summed in bfloat16 or wider, within the bound.
A program may use at most 256 MiB of HBM per device.

v0:
```python
import jax
import jax.numpy as jnp
from jax import lax
from jax.sharding import PartitionSpec as P

learn_rate = 0.002
beta_one = 0.9
beta_two = 0.999
adam_eps = 1e-08
weight_decay = 0.1
clip_norm = 1.0
decay_rate = 0.99


def adam_update(param, first, second, gradient, time, decay):
    first_new = beta_one * first + (1.0 - beta_one) * gradient
    second_new = beta_two * second + (1.0 - beta_two) * gradient * gradient
    bias_one = 1.0 - jnp.power(jnp.float32(beta_one), time)
    bias_two = 1.0 - jnp.power(jnp.float32(beta_two), time)
    ratio = first_new / bias_one / (jnp.sqrt(second_new / bias_two) + adam_eps)
    param_new = param - learn_rate * (ratio + decay * param)
    return (param_new, first_new, second_new)


def shards(
    grads,
    small_grads,
    counts,
    step,
    master,
    moment_one,
    moment_two,
    average,
    small_master,
    small_one,
    small_two,
    small_average,
):
    micro = grads.shape[0]
    valid = (jnp.arange(micro, dtype=jnp.int32) < counts[0]).astype(jnp.float32)
    big_term = valid[0] * grads[0].astype(jnp.float32)
    small_term = valid[0] * small_grads[0].astype(jnp.float32)
    big_term = big_term + valid[1] * grads[1].astype(jnp.float32)
    small_term = small_term + valid[1] * small_grads[1].astype(jnp.float32)
    big_rows, small_part = (
        lax.psum_scatter(big_term, "shard", scatter_dimension=0, tiled=True),
        lax.psum_scatter(small_term, "shard", scatter_dimension=0, tiled=True),
    )
    flat_sum = lax.all_to_all(big_rows, "tensor", split_axis=0, concat_axis=1, tiled=True)
    small_part = small_part.reshape(1, -1)
    local_squares = jnp.sum(big_rows * big_rows) + jnp.sum(small_part * small_part)
    squares = lax.psum(local_squares, ("shard", "tensor"))
    norm = jnp.sqrt(squares)
    factor = jnp.minimum(1.0, clip_norm / (norm + 1e-06))
    time = step[0].astype(jnp.float32)
    new_master, new_one, new_two = adam_update(
        master, moment_one, moment_two, flat_sum * factor, time, weight_decay
    )
    small_new, small_new_one, small_new_two = adam_update(
        small_master, small_one, small_two, small_part * factor, time, 0.0
    )
    new_average = decay_rate * average + (1.0 - decay_rate) * new_master
    small_new_average = decay_rate * small_average + (1.0 - decay_rate) * small_new
    weights_flat = new_master.astype(jnp.bfloat16)
    small_weights = small_new.astype(jnp.bfloat16)
    weight_parts = lax.all_to_all(weights_flat, "tensor", split_axis=1, concat_axis=0, tiled=True)
    weight_blocks, small_all = (
        lax.all_gather(weight_parts, "shard", axis=0, tiled=True),
        lax.all_gather(small_weights, "shard", axis=1, tiled=True),
    )
    average_parts = lax.all_to_all(new_average, "tensor", split_axis=1, concat_axis=0, tiled=True)
    average_blocks, small_average_all = (
        lax.all_gather(average_parts, "shard", axis=0, tiled=True),
        lax.all_gather(small_new_average, "shard", axis=1, tiled=True),
    )
    return (
        new_master,
        new_one,
        new_two,
        small_new,
        small_new_one,
        small_new_two,
        weight_blocks,
        small_all.reshape(-1),
        average_blocks,
        small_average_all.reshape(-1),
    )


def solution(mesh):
    placed = (
        P("shard", None, "tensor"),
        P("shard", "tensor"),
        P("shard"),
        P(),
        P(("shard", "tensor"), None),
        P(("shard", "tensor"), None),
        P(("shard", "tensor"), None),
        P(("shard", "tensor"), None),
        P("tensor", "shard"),
        P("tensor", "shard"),
        P("tensor", "shard"),
        P("tensor", "shard"),
    )
    return jax.shard_map(
        shards,
        mesh=mesh,
        in_specs=placed,
        out_specs=(
            P(("shard", "tensor"), None),
            P(("shard", "tensor"), None),
            P(("shard", "tensor"), None),
            P("tensor", "shard"),
            P("tensor", "shard"),
            P("tensor", "shard"),
            P(None, "tensor"),
            P("tensor"),
            P(None, "tensor"),
            P("tensor"),
        ),
        check_vma=False,
    )
```

profile of v0, /device:TPU:1, one launch (start us, length us, event | category | flops | bytes accessed | tf_op | source)
XLA Modules:
  0.0 416.9 jit_solution(6151699952216724307)
XLA Ops:
  7.9 0.6 fusion.6
  8.5 8.8 %add_bitcast_fusion = f32[896,2080]{0,1:T(8,128)} fusion(bf16[2,896,2080]{1,2,0:T(8,128)(2,1)} %param.12, f32[]{:T(128)} %bitcast.4, f32[]{:T(128)} %bitcast.3), kind=kLoop, calls=%fused_computation | loop fusion | flops 9318400 | bytes 14909448 | tf_op jit(solution)/shard_map/add | solution.py:43
  17.3 0.6 copy-done.5
  17.9 0.6 fusion.5
  19.1 134.4 %all-reduce.6.cloned.1.call-done = f32[896,2080]{0,1:T(8,128)} async-done(((f32[896,2080]{0,1:T(8,128)}), f32[896,2080]{0,1:T(8,128)}) %all-reduce.6.cloned.1.call-update) | async-done | bytes 7454736
  153.5 2.5 multiply_reduce_fusion
  156.4 0.9 all_to_all.38
  157.3 4.9 %all-to-all-start = ((f32[8,7,2080]{2,1,0:T(8,128)}), f32[8,7,2080]{2,1,0:T(8,128)S(1)}, u32[]{:S(2)}, u32[]{:S(2)}) async-start(f32[8,7,2080]{2,1,0:T(8,128)} %all_to_all.38), calls=%async_computation | async-start | bytes 1114112 | tf_op jit(solution)/shard_map/all_to_all | solution.py:49
  163.6 1.3 add_reduce_fusion
  164.9 30.9 %all-reduce.3 = f32[368]{0:T(512)S(1)} all-reduce(f32[368]{0:T(512)S(1)} %add_reduce_fusion), channel_id=3, replica_groups=mesh['shard'=16,'tensor'=8] {'shard'}, use_global_device_ids=true, to_apply=%region_2.0.clone | all-reduce | flops 368 | bytes 2944
  195.8 0.7 multiply_reduce_fusion.1
  197.8 69.7 %psum.7 = f32[]{:T(128)} all-reduce(f32[]{:T(128)S(6)} %add.61), channel_id=1, replica_groups=mesh['shard'=16,'tensor'=8] {'shard','tensor'}, use_global_device_ids=true, to_apply=%region_4.0 | all-reduce | flops 1 | bytes 8 | tf_op jit(solution)/shard_map/psum | solution.py:52
  268.7 2.5 multiply_add_fusion
  271.2 0.5 all_to_all.40
  271.7 11.8 %all_to_all.51 = bf16[7,8,2080]{2,0,1:T(8,128)(2,1)S(1)} all-to-all(bf16[7,8,2080]{2,0,1:T(8,128)(2,1)S(1)} %copy.38), channel_id=1, replica_groups=mesh['shard'=16,'tensor'=8] {'tensor'}, dimensions={1} | all-to-all | bytes 465920 | tf_op jit(solution)/shard_map/all_to_all | solution.py:66
  283.6 0.8 all_to_all.43
  285.0 13.0 %all_to_all.52 = f32[7,8,2080]{2,0,1:T(8,128)S(1)} all-to-all(f32[7,8,2080]{2,0,1:T(8,128)S(1)} %copy.39), channel_id=1, replica_groups=mesh['shard'=16,'tensor'=8] {'tensor'}, dimensions={1} | all-to-all | bytes 931840 | tf_op jit(solution)/shard_map/all_to_all | solution.py:71
  298.1 0.8 all_to_all.47
  299.6 0.6 bitcast_dynamic-update-slice_fusion
  300.5 30.7 %all-reduce = bf16[368]{0:T(512)(128)(2,1)} all-reduce(bf16[368]{0:T(512)(128)(2,1)S(1)} %dynamic-update-slice), channel_id=1, replica_groups=mesh['shard'=16,'tensor'=8] {'shard'}, use_global_device_ids=true, to_apply=%add | all-reduce | flops 368 | bytes 1472 | tf_op jit(solution)/shard_map/reshape | solution.py:84
  331.2 30.5 %all-reduce.1 = f32[368]{0:T(512)} all-reduce(f32[368]{0:T(512)S(1)} %get-tuple-element.40), channel_id=1, replica_groups=mesh['shard'=16,'tensor'=8] {'shard'}, use_global_device_ids=true, to_apply=%add.1 | all-reduce | flops 368 | bytes 2944 | tf_op jit(solution)/shard_map/reshape | solution.py:86
  361.7 6.1 %copy.40 = bf16[896,2080]{0,1:T(8,128)(2,1)} copy(bf16[896,2080]{1,0:T(8,128)(2,1)} %all-gather.3.cloned.1.call-done) | data formatting | bytes 7454720
  367.8 34.0 %all-gather.5.cloned.1.call-done = f32[896,2080]{1,0:T(8,128)} async-done(((f32[56,2080]{1,0:T(8,128)}), f32[896,2080]{1,0:T(8,128)}) %all-gather.5.cloned.1.call-update) | async-done | bytes 7454736 | tf_op jit(solution)/shard_map/all_gather | solution.py:73
  401.8 8.6 %copy.41 = f32[896,2080]{0,1:T(8,128)} copy(f32[896,2080]{1,0:T(8,128)} %all-gather.5.cloned.1.call-done) | data formatting | bytes 14909440
  (42 shorter events, 1.8 us)
Async XLA Ops:
  7.2 146.3 %all-reduce.6.cloned.1.call-start = ((), (), s32[]{:S(2)}) async-start(), calls=%async_computation.5 | async-start | bytes 14909440
  17.2 0.7 copy-start.5
  17.2 146.3 %copy-start.4 = (bf16[2,368]{1,0:T(2,128)(2,1)S(1)}, bf16[2,368]{1,0:T(2,128)(2,1)}, u32[]{:S(2)}) copy-start(bf16[2,368]{1,0:T(2,128)(2,1)} %param.13) | copy-start | bytes 4420
  17.2 251.5 %copy-start.1 = (f32[7,16640]{1,0:T(8,128)S(1)}, f32[7,16640]{1,0:T(8,128)}, u32[]{:S(2)}) copy-start(f32[7,16640]{1,0:T(8,128)} %param.19) | copy-start | bytes 1397764
  17.2 251.5 %copy-start.2 = (f32[7,16640]{1,0:T(8,128)S(1)}, f32[7,16640]{1,0:T(8,128)}, u32[]{:S(2)}) copy-start(f32[7,16640]{1,0:T(8,128)} %param.16) | copy-start | bytes 1397764
  17.2 251.5 %copy-start.3 = (f32[7,16640]{1,0:T(8,128)S(1)}, f32[7,16640]{1,0:T(8,128)}, u32[]{:S(2)}) copy-start(f32[7,16640]{1,0:T(8,128)} %param.18) | copy-start | bytes 1397764
  157.3 111.0 %all-to-all-start = ((f32[8,7,2080]{2,1,0:T(8,128)}), f32[8,7,2080]{2,1,0:T(8,128)S(1)}, u32[]{:S(2)}, u32[]{:S(2)}) async-start(f32[8,7,2080]{2,1,0:T(8,128)} %all_to_all.38), calls=%async_computation | async-start | bytes 1114112 | tf_op jit(solution)/shard_map/all_to_all | solution.py:49
  162.2 199.5 %all-gather.3.cloned.1.call-start = ((), (), s32[]{:S(2)}) async-start(), calls=%async_computation.3 | async-start | bytes 4143104 | tf_op jit(solution)/shard_map/all_gather | solution.py:68
  268.3 31.3 %copy-start.6 = (f32[1,23]{1,0:T(1,128)S(1)}, f32[1,23]{1,0:T(1,128)}, u32[]{:S(2)}) copy-start(f32[1,23]{1,0:T(1,128)} %param.23) | copy-start | bytes 280
  268.3 31.3 %copy-start.7 = (f32[1,23]{1,0:T(1,128)S(1)}, f32[1,23]{1,0:T(1,128)}, u32[]{:S(2)}) copy-start(f32[1,23]{1,0:T(1,128)} %param.20) | copy-start | bytes 280
  268.3 31.3 %copy-start.8 = (f32[1,23]{1,0:T(1,128)S(1)}, f32[1,23]{1,0:T(1,128)}, u32[]{:S(2)}) copy-start(f32[1,23]{1,0:T(1,128)} %param.22) | copy-start | bytes 280
  268.3 31.3 %copy-start.9 = (f32[1,23]{1,0:T(1,128)S(1)}, f32[1,23]{1,0:T(1,128)}, u32[]{:S(2)}) copy-start(f32[1,23]{1,0:T(1,128)} %param.21) | copy-start | bytes 280
  271.2 96.6 %copy-start = (f32[7,16640]{1,0:T(8,128)}, f32[7,16640]{1,0:T(8,128)S(1)}, u32[]{:S(2)}) copy-start(f32[7,16640]{1,0:T(8,128)S(1)} %get-tuple-element.45) | copy-start | bytes 1397764
  284.4 117.4 %all-gather.5.cloned.1.call-start = ((), (), s32[]{:S(2)}) async-start(), calls=%async_computation.4 | async-start | bytes 8286208 | tf_op jit(solution)/shard_map/all_gather | solution.py:73
  300.2 110.1 %copy-start.10 = (f32[1,23]{1,0:T(1,128)}, f32[1,23]{1,0:T(1,128)S(1)}, u32[]{:S(2)}) copy-start(f32[1,23]{1,0:T(1,128)S(1)} %get-tuple-element.41) | copy-start | bytes 280
Sparse Core Ops, SparseCore 0:
  17.4 136.0 all-reduce.5
  284.6 46.2 all-gather.2
  333.9 67.8 all-gather.4
where the time goes:
time: 418 us; the launch traced here: 417 us
  blocking collectives  187 us (45%)
  waiting for transfers between devices  168 us (40%)
  local copies, waits for them, and re-layouts  21.1 us (5%)
  between operations  19.3 us (5%)
  other arithmetic  16.5 us (4%)
  starting transfers between devices  5.01 us (1%)
    unnamed x4, waiting for transfers between devices  134 us
    psum x1, blocking collectives, shards(): squares = lax.psum(local_squares, ('shard', 'tensor'))  69.7 us
    all_gather x1, waiting for transfers between devices, shards(): lax.all_gather(average_parts, 'shard', axis=0, tiled=True)  34 us
    unnamed x1, blocking collectives  30.9 us
    reshape x1, blocking collectives, shards(): small_all.reshape(-1)  30.7 us
    reshape x1, blocking collectives, shards(): small_average_all.reshape(-1)  30.5 us
    unnamed x28, local copies, waits for them, and re-layouts  16.2 us
    all_to_all x1, blocking collectives, shards(): lax.all_to_all(new_average, 'tensor', split_axis=1, concat_axis=0, tiled=...  13 us
  transfers between devices with their start and end apart: 4, of which 2 were waited for; matrix products, arithmetic and copies ran while one was open for 2% of the time, Pallas kernels for 0%

commit v1 on v0

v1 whole, which is shorter than its diff:
```python
import jax
import jax.numpy as jnp
from jax import lax
from jax.experimental import pallas as pl
from jax.experimental.pallas import tpu as pltpu
from jax.sharding import PartitionSpec as P

learn_rate = 0.002
beta_one = 0.9
beta_two = 0.999
adam_eps = 1e-08
weight_decay = 0.1
clip_norm = 1.0
decay_rate = 0.99

MESH = pl.DeviceIdType.MESH
RING = 4
SHARDS = RING * RING
TENSORS = 8
ROWS = 56
MINE = 7
COLS = 2080
ALL_COLS = COLS * TENSORS
SMALL = 368
SEG = 23
LANES = 384
PARTS = ((0, 512), (512, 512), (1024, 512), (1536, 544))
TOP = 32700.0
SUM_MAX = 2.0
AVERAGE_MAX = 0.03


def encode(x, most):
    scaled = jnp.abs(x) * (TOP**4 / most) + 1e-20
    root = (lax.rsqrt(lax.rsqrt(scaled)) + 0.5).astype(jnp.int32)
    return jnp.where(x < 0.0, -root, root).astype(jnp.int16)


def decode(code, most):
    root = code.astype(jnp.int32).astype(jnp.float32)
    return (root * root) * (root * jnp.abs(root)) * (most / TOP**4)


def adam(param, first, second, gradient, bias_one, bias_two, decay):
    first_new = beta_one * first + (1.0 - beta_one) * gradient
    second_new = beta_two * second + (1.0 - beta_two) * gradient * gradient
    ratio = first_new / bias_one / (jnp.sqrt(second_new / bias_two) + adam_eps)
    return param - learn_rate * (ratio + decay * param), first_new, second_new


def wrap(position, shift, size):
    return lax.rem(position + (shift + size), size)


def step_kernel(
    scal,
    small_in,
    grads_hbm,
    master_hbm,
    one_hbm,
    two_hbm,
    average_hbm,
    master_out,
    one_out,
    two_out,
    small_out,
    weights_out,
    codes_out,
    gv,
    pm,
    p1,
    p2,
    pa,
    om,
    o1,
    o2,
    big_send,
    big_recv,
    kept,
    mid_send,
    mid_recv,
    total,
    chunk_send,
    chunk_recv,
    wchunk_send,
    wchunk_recv,
    achunk_send,
    achunk_recv,
    norm_send,
    norm_t,
    norm_y,
    norm_z,
    small_send,
    small_y,
    small_z,
    wall,
    aall,
    load_sem,
    store_sem,
    rs_send_sem,
    rs_recv_sem,
    t_send_sem,
    t_recv_sem,
    r_send_sem,
    r_recv_sem,
    ag_send_sem,
    ag_recv_sem,
):
    s = lax.axis_index("shard")
    t = lax.axis_index("tensor")
    pos = (lax.div(s, RING), lax.rem(s, RING))
    core_sign = 1 - 2 * lax.rem(t, 2)

    def ring_device(axis, p):
        return (p * RING + pos[1], t) if axis == 0 else (pos[0] * RING + p, t)

    def shard_of(axis, p, k):
        return p * RING + k if axis == 0 else k * RING + p

    loads = []
    for i, (src, dst) in enumerate(
        ((grads_hbm, gv), (master_hbm, pm), (one_hbm, p1), (two_hbm, p2), (average_hbm, pa))
    ):
        load = pltpu.make_async_copy(src, dst, load_sem.at[i])
        load.start()
        loads.append(load)

    barrier = pltpu.get_barrier_semaphore()
    for axis in range(2):
        for d in range(1, RING):
            pl.semaphore_signal(
                barrier, inc=1, device_id=ring_device(axis, wrap(pos[axis], d, RING)), device_id_type=MESH
            )
    for d in range(1, TENSORS):
        pl.semaphore_signal(barrier, inc=1, device_id=(s, wrap(t, d, TENSORS)), device_id_type=MESH)
    pl.semaphore_wait(barrier, 2 * (RING - 1) + TENSORS - 1)

    pending = []

    def send(src, dst, send_sem, recv_sem, device):
        copy = pltpu.make_async_remote_copy(
            src_ref=src, dst_ref=dst, send_sem=send_sem, recv_sem=recv_sem, device_id=device, device_id_type=MESH
        )
        copy.start()
        pending.append(copy)
        return copy

    def ring_share(kind, axis, src, dst):
        return [
            send(
                src,
                dst.at[d - 1],
                r_send_sem.at[kind, d - 1],
                r_recv_sem.at[kind, d - 1],
                ring_device(axis, wrap(pos[axis], d, RING)),
            )
            for d in range(1, RING)
        ]

    small_copies = ring_share(0, 0, small_in, small_y)
    loads[0].wait()
    valid_one, valid_two = scal[0], scal[1]

    def local(shard, q):
        first, width = PARTS[q]
        a = gv[0, shard, :, pl.ds(first, width)].astype(jnp.float32)
        b = gv[1, shard, :, pl.ds(first, width)].astype(jnp.float32)
        return valid_one * a + valid_two * b

    axes = ((0, 1), (0, 1), (1, 0), (1, 0))
    signs = (core_sign, -core_sign, core_sign, -core_sign)
    order = [[wrap(pos[axes[q][1]], k, RING) for k in (2, signs[q], -signs[q], 0)] for q in range(4)]
    early = [[None] * 2 for _ in range(4)]
    for slot in range(2):
        for q in range(4):
            axis, sign = axes[q][0], signs[q]
            p = pos[axis]
            dest = wrap(p, 2, RING) if slot == 0 else wrap(p, sign, RING)

            def fill(k, carry, q=q, axis=axis, dest=dest, slot=slot):
                big_send[q][slot, k] = encode(local(shard_of(axis, dest, k), q), SUM_MAX)
                return carry

            lax.fori_loop(0, RING, fill, 0)
            to = wrap(p, -sign, RING) if slot == 0 else dest
            early[q][slot] = send(
                big_send[q].at[slot],
                big_recv[q].at[slot],
                rs_send_sem.at[q, slot],
                rs_recv_sem.at[q, slot],
                ring_device(axis, to),
            )
    relayed = [[None] * RING for _ in range(4)]
    for q in range(4):
        early[q][0].wait_recv()
    for i in range(RING):
        for q in range(4):
            axis, sign = axes[q][0], signs[q]
            dest = wrap(pos[axis], -sign, RING)
            k = order[q][i]
            came = decode(big_recv[q][0, k], SUM_MAX)
            big_send[q][2, k] = encode(local(shard_of(axis, dest, k), q) + came, 2 * SUM_MAX)
            relayed[q][i] = send(
                big_send[q].at[2, k],
                big_recv[q].at[2, k],
                rs_send_sem.at[q, 2 + i],
                rs_recv_sem.at[q, 2 + i],
                ring_device(axis, dest),
            )
    for copy in small_copies:
        copy.wait_recv()
    small_send[...] = small_in[...] + small_y[0] + small_y[1] + small_y[2]
    small_copies = ring_share(1, 1, small_send, small_z)
    for q in range(4):
        early[q][1].wait_recv()

    later = [[None] * 3 for _ in range(4)]
    for i in range(RING):
        for q in range(4):
            (axis, other), sign = axes[q], signs[q]
            k = order[q][i]
            relayed[q][i].wait_recv()
            piece = (
                local(shard_of(axis, pos[axis], k), q)
                + decode(big_recv[q][1, k], SUM_MAX)
                + decode(big_recv[q][2, k], 2 * SUM_MAX)
            )
            if i >= 2:
                kept[q][i - 2] = piece
                continue
            mid_send[q][i] = encode(piece, 4 * SUM_MAX)
            to = wrap(pos[other], -sign if i == 0 else sign, RING)
            later[q][i] = send(
                mid_send[q].at[i],
                mid_recv[q].at[i],
                rs_send_sem.at[q, 6 + i],
                rs_recv_sem.at[q, 6 + i],
                ring_device(other, to),
            )
    for q in range(4):
        other, sign = axes[q][1], signs[q]
        later[q][0].wait_recv()
        mid_send[q][2] = encode(kept[q][0] + decode(mid_recv[q][0], 4 * SUM_MAX), 8 * SUM_MAX)
        later[q][2] = send(
            mid_send[q].at[2],
            mid_recv[q].at[2],
            rs_send_sem.at[q, 8],
            rs_recv_sem.at[q, 8],
            ring_device(other, wrap(pos[other], -sign, RING)),
        )
    for copy in small_copies:
        copy.wait_recv()
    small_all = small_send[...] + small_z[0] + small_z[1] + small_z[2]
    small_sum = small_all[0:1]
    squares = jnp.sum(small_sum * small_sum) * (1.0 / SHARDS)
    for q in range(4):
        first, width = PARTS[q]
        later[q][1].wait_recv()
        later[q][2].wait_recv()
        piece = kept[q][1] + decode(mid_recv[q][1], 4 * SUM_MAX) + decode(mid_recv[q][2], 8 * SUM_MAX)
        total[:, pl.ds(first, width)] = piece
        squares = squares + jnp.sum(piece * piece)

    norm_send[0] = jnp.full((8, 128), squares, jnp.float32)
    norm_copies = []
    for d in range(1, TENSORS):
        norm_copies.append(
            send(
                norm_send.at[0],
                norm_t.at[d - 1],
                t_send_sem.at[0, d],
                t_recv_sem.at[0, d],
                (s, wrap(t, d, TENSORS)),
            )
        )
    for j in range(TENSORS):
        chunk_send[j] = encode(total[pl.ds(MINE * j, MINE), :], 16 * SUM_MAX)
    chunk_recv[t] = chunk_send[t]

    def exchange(kind, src, dst):
        copies = []
        for d in range(1, TENSORS):
            to = wrap(t, d, TENSORS)
            copies.append(
                send(src.at[to], dst.at[t], t_send_sem.at[kind, d], t_recv_sem.at[kind, d], (s, to))
            )
        return copies

    chunk_copies = exchange(1, chunk_send, chunk_recv)
    for copy in norm_copies:
        copy.wait_recv()
    norm = norm_send[0]
    for d in range(TENSORS - 1):
        norm = norm + norm_t[d]
    norm_send[1] = norm
    for copy in ring_share(2, 0, norm_send.at[1], norm_y):
        copy.wait_recv()
    norm = norm_send[1] + norm_y[0] + norm_y[1] + norm_y[2]
    norm_send[2] = norm
    for copy in ring_share(3, 1, norm_send.at[2], norm_z):
        copy.wait_recv()
    norm = jnp.sqrt(norm_send[2] + norm_z[0] + norm_z[1] + norm_z[2])
    factor = jnp.minimum(1.0, clip_norm / (norm + 1e-06))[0:1, 0:1]

    bias_one, bias_two = scal[2], scal[3]
    for load in loads[1:]:
        load.wait()
    for copy in chunk_copies:
        copy.wait_recv()
    half = ALL_COLS // 2
    for h in range(2):
        cols = pl.ds(half * h, half)
        summed = jnp.concatenate([decode(chunk_recv[4 * h + j], 16 * SUM_MAX) for j in range(4)], axis=1)
        new, one, two = adam(pm[:, cols], p1[:, cols], p2[:, cols], summed * factor, bias_one, bias_two, weight_decay)
        om[:, cols] = new
        o1[:, cols] = one
        o2[:, cols] = two
        smooth = decay_rate * pa[:, cols] + (1.0 - decay_rate) * new
        for j in range(4):
            wchunk_send[4 * h + j] = new[:, COLS * j : COLS * (j + 1)].astype(jnp.bfloat16)
            achunk_send[4 * h + j] = encode(smooth[:, COLS * j : COLS * (j + 1)], AVERAGE_MAX)
    wchunk_recv[t] = wchunk_send[t]
    achunk_recv[t] = achunk_send[t]
    wchunk_copies = exchange(2, wchunk_send, wchunk_recv)
    achunk_copies = exchange(3, achunk_send, achunk_recv)
    stores = []
    for i, (src, dst) in enumerate(((om, master_out), (o1, one_out), (o2, two_out))):
        store = pltpu.make_async_copy(src, dst, store_sem.at[i])
        store.start()
        stores.append(store)

    new, one, two = adam(
        small_all[1:2], small_all[2:3], small_all[3:4], small_sum * factor, bias_one, bias_two, 0.0
    )
    smooth = decay_rate * small_all[4:5] + (1.0 - decay_rate) * new
    small_out[0:1] = new
    small_out[1:2] = one
    small_out[2:3] = two
    small_out[3:4] = smooth
    small_out[4:8] = jnp.zeros((4, LANES), jnp.float32)

    for copy in wchunk_copies:
        copy.wait_recv()
    rows = jnp.concatenate([wchunk_recv[j].astype(jnp.float32) for j in range(TENSORS)], axis=0)
    wall[s] = rows.astype(jnp.bfloat16)
    for copy in achunk_copies:
        copy.wait_recv()
    rows = jnp.concatenate([achunk_recv[j].astype(jnp.int32) for j in range(TENSORS)], axis=0)
    aall[s] = rows.astype(jnp.int16)

    arrays = (wall, aall)
    lanes = [(x, q) for x in range(2) for q in range(4)]

    def gather_send(x, q, shard, index, axis, sign):
        first, width = PARTS[q]
        ref = arrays[x].at[shard, :, pl.ds(first, width)]
        send(
            ref,
            ref,
            ag_send_sem.at[x, q, index],
            ag_recv_sem.at[x, q, index],
            ring_device(axis, wrap(pos[axis], sign, RING)),
        )

    def gather_wait(x, q, shard, index):
        first, width = PARTS[q]
        ref = arrays[x].at[shard, :, pl.ds(first, width)]
        pltpu.make_async_remote_copy(
            src_ref=ref,
            dst_ref=ref,
            send_sem=ag_send_sem.at[x, q, index],
            recv_sem=ag_recv_sem.at[x, q, index],
            device_id=ring_device(0, wrap(pos[0], 1, RING)),
            device_id_type=MESH,
        ).wait_recv()

    def outer(x, q, j, shard):
        axis, sign = axes[q][0], signs[q]
        gather_send(x, q, shard, 3 + 3 * j, axis, sign)
        gather_send(x, q, shard, 4 + 3 * j, axis, -sign)

    def source(q, shift, shift_outer):
        axis, other = axes[q]
        return shard_of(axis, wrap(pos[axis], shift_outer, RING), wrap(pos[other], shift, RING))

    def relay(x, q, j, shift):
        axis, sign = axes[q][0], signs[q]
        shard = source(q, shift, -sign)
        gather_wait(x, q, shard, 3 + 3 * j)
        gather_send(x, q, shard, 5 + 3 * j, axis, sign)

    for x, q in lanes:
        other, sign = axes[q][1], signs[q]
        gather_send(x, q, s, 0, other, sign)
        gather_send(x, q, s, 1, other, -sign)
        outer(x, q, 0, s)
    for x, q in lanes:
        other, sign = axes[q][1], signs[q]
        shard = source(q, -sign, 0)
        gather_wait(x, q, shard, 0)
        gather_send(x, q, shard, 2, other, sign)
        outer(x, q, 1, shard)
        relay(x, q, 0, 0)
    for x, q in lanes:
        sign = signs[q]
        shard = source(q, sign, 0)
        gather_wait(x, q, shard, 1)
        outer(x, q, 2, shard)
        relay(x, q, 1, -sign)
    for x, q in lanes:
        sign = signs[q]
        shard = source(q, 2, 0)
        gather_wait(x, q, shard, 2)
        outer(x, q, 3, shard)
        relay(x, q, 2, sign)
    for x, q in lanes:
        relay(x, q, 3, 2)
    for x, q in lanes:
        sign = signs[q]
        for j, shift in enumerate((0, -sign, sign, 2)):
            gather_wait(x, q, source(q, shift, sign), 4 + 3 * j)
            gather_wait(x, q, source(q, shift, 2), 5 + 3 * j)
    for i, (src, dst) in enumerate(((wall, weights_out), (aall, codes_out))):
        store = pltpu.make_async_copy(src, dst, store_sem.at[3 + i])
        store.start()
        stores.append(store)
    for copy in pending:
        copy.wait_send()
    for store in stores:
        store.wait()


def communicate(scal, small_in, grads, master, one, two, average):
    hbm = pl.BlockSpec(memory_space=pl.ANY)
    vmem = pl.BlockSpec(memory_space=pltpu.VMEM)
    f32, bf16, i16 = jnp.float32, jnp.bfloat16, jnp.int16
    rows = jax.ShapeDtypeStruct((MINE, ALL_COLS), f32)
    widths = [w for _, w in PARTS]
    chunk = (TENSORS, MINE, COLS)
    return pl.pallas_call(
        step_kernel,
        out_shape=(
            rows,
            rows,
            rows,
            jax.ShapeDtypeStruct((8, LANES), f32),
            jax.ShapeDtypeStruct((SHARDS, ROWS, COLS), bf16),
            jax.ShapeDtypeStruct((SHARDS, ROWS, COLS), i16),
        ),
        in_specs=[pl.BlockSpec(memory_space=pltpu.SMEM), vmem] + [hbm] * 5,
        out_specs=(hbm, hbm, hbm, vmem, hbm, hbm),
        scratch_shapes=[
            pltpu.VMEM((2, SHARDS, ROWS, COLS), bf16),
            *[pltpu.VMEM((MINE, ALL_COLS), f32)] * 7,
            [pltpu.VMEM((3, RING, ROWS, w), i16) for w in widths],
            [pltpu.VMEM((3, RING, ROWS, w), i16) for w in widths],
            [pltpu.VMEM((2, ROWS, w), f32) for w in widths],
            [pltpu.VMEM((3, ROWS, w), i16) for w in widths],
            [pltpu.VMEM((3, ROWS, w), i16) for w in widths],
            pltpu.VMEM((ROWS, COLS), f32),
            pltpu.VMEM(chunk, i16),
            pltpu.VMEM(chunk, i16),
            pltpu.VMEM(chunk, bf16),
            pltpu.VMEM(chunk, bf16),
            pltpu.VMEM(chunk, i16),
            pltpu.VMEM(chunk, i16),
            pltpu.VMEM((3, 8, 128), f32),
            pltpu.VMEM((TENSORS - 1, 8, 128), f32),
            pltpu.VMEM((RING - 1, 8, 128), f32),
            pltpu.VMEM((RING - 1, 8, 128), f32),
            pltpu.VMEM((8, LANES), f32),
            pltpu.VMEM((RING - 1, 8, LANES), f32),
            pltpu.VMEM((RING - 1, 8, LANES), f32),
            pltpu.VMEM((SHARDS, ROWS, COLS), bf16),
            pltpu.VMEM((SHARDS, ROWS, COLS), i16),
            pltpu.SemaphoreType.DMA((5,)),
            pltpu.SemaphoreType.DMA((5,)),
            pltpu.SemaphoreType.DMA((4, 9)),
            pltpu.SemaphoreType.DMA((4, 9)),
            pltpu.SemaphoreType.DMA((4, TENSORS)),
            pltpu.SemaphoreType.DMA((4, TENSORS)),
            pltpu.SemaphoreType.DMA((4, RING - 1)),
            pltpu.SemaphoreType.DMA((4, RING - 1)),
            pltpu.SemaphoreType.DMA((2, 4, 15)),
            pltpu.SemaphoreType.DMA((2, 4, 15)),
        ],
        compiler_params=pltpu.CompilerParams(
            collective_id=0, has_side_effects=True, vmem_limit_bytes=60 * 1024 * 1024
        ),
        name="step",
    )(scal, small_in, grads, master, one, two, average)


def finish_kernel(weights, codes, master, one, two, weights_out, average_out, master_out, one_out, two_out):
    weights_out[...] = weights[...]
    average_out[...] = decode(codes[...], AVERAGE_MAX)

    @pl.when(pl.program_id(0) == 0)
    def _():
        master_out[...] = master[...]
        one_out[...] = one[...]
        two_out[...] = two[...]


def finish(weights, codes, master, one, two):
    block = pl.BlockSpec((2, ROWS, COLS), lambda i: (i, 0, 0))
    whole = pl.BlockSpec((MINE, ALL_COLS), lambda i: (0, 0))
    rows = jax.ShapeDtypeStruct((MINE, ALL_COLS), jnp.float32)
    return pl.pallas_call(
        finish_kernel,
        grid=(SHARDS // 2,),
        in_specs=[block, block, whole, whole, whole],
        out_specs=[block, block, whole, whole, whole],
        out_shape=(
            jax.ShapeDtypeStruct((SHARDS, ROWS, COLS), jnp.bfloat16),
            jax.ShapeDtypeStruct((SHARDS, ROWS, COLS), jnp.float32),
            rows,
            rows,
            rows,
        ),
        name="finish",
    )(weights, codes, master, one, two)


def shards(
    grads,
    small_grads,
    counts,
    step,
    master,
    moment_one,
    moment_two,
    average,
    small_master,
    small_one,
    small_two,
    small_average,
):
    s = lax.axis_index("shard")
    valid = (jnp.arange(2, dtype=jnp.int32) < counts[0]).astype(jnp.float32)
    time = step[0].astype(jnp.float32)
    bias_one = 1.0 - jnp.power(jnp.float32(beta_one), time)
    bias_two = 1.0 - jnp.power(jnp.float32(beta_two), time)
    scal = jnp.stack([valid[0], valid[1], bias_one, bias_two])
    small_term = valid[0] * small_grads[0].astype(jnp.float32) + valid[1] * small_grads[1].astype(jnp.float32)
    state = jnp.concatenate([small_master, small_one, small_two, small_average], axis=0)
    small_in = jnp.zeros((8, LANES), jnp.float32)
    small_in = lax.dynamic_update_slice(small_in, small_term[None], (0, 0))
    small_in = lax.dynamic_update_slice(small_in, state, (1, SEG * s))
    new_master, new_one, new_two, small_new, weights, codes = communicate(
        scal, small_in, grads.reshape(2, SHARDS, ROWS, COLS), master, moment_one, moment_two, average
    )
    weights, averages, new_master, new_one, new_two = finish(weights, codes, new_master, new_one, new_two)
    mine = lax.dynamic_slice(small_new, (0, SEG * s), (3, SEG))
    return (
        new_master,
        new_one,
        new_two,
        mine[0:1],
        mine[1:2],
        mine[2:3],
        weights.reshape(SHARDS * ROWS, COLS),
        small_new[0, :SMALL].astype(jnp.bfloat16),
        averages.reshape(SHARDS * ROWS, COLS),
        small_new[3, :SMALL],
    )


def solution(mesh):
    placed = (
        P("shard", None, "tensor"),
        P("shard", "tensor"),
        P("shard"),
        P(),
        P(("shard", "tensor"), None),
        P(("shard", "tensor"), None),
        P(("shard", "tensor"), None),
        P(("shard", "tensor"), None),
        P("tensor", "shard"),
        P("tensor", "shard"),
        P("tensor", "shard"),
        P("tensor", "shard"),
    )
    return jax.shard_map(
        shards,
        mesh=mesh,
        in_specs=placed,
        out_specs=(
            P(("shard", "tensor"), None),
            P(("shard", "tensor"), None),
            P(("shard", "tensor"), None),
            P("tensor", "shard"),
            P("tensor", "shard"),
            P("tensor", "shard"),
            P(None, "tensor"),
            P("tensor"),
            P(None, "tensor"),
            P("tensor"),
        ),
        check_vma=False,
    )
```

time: 418 us -> 154 us (0.37)
  blocking collectives: 187 us -> 0 us
  waiting for transfers between devices: 168 us -> 0 us
  Pallas kernels: 0 us -> 116 us
  between operations: 19.3 us -> 2.06 us
  other arithmetic: 16.5 us -> 3.36 us
  local copies, waits for them, and re-layouts: 21.1 us -> 31.1 us
  starting transfers between devices: 5.01 us -> 0 us
    unnamed x4 -> x0, waiting for transfers between devices: 134 us -> none
    pallas_call x0 -> x2, Pallas kernels: none -> 116 us  [the longest x1 105 us: communicate(): pl.pallas_call(step_kernel, out_shape=(rows, rows, rows, jax.ShapeDtypeSt...]
    psum x1 -> x0, blocking collectives: 69.7 us -> none  [shards(): squares = lax.psum(local_squares, ('shard', 'tensor'))]
    reshape x2 -> x0, blocking collectives: 61.2 us -> none  [the longest x1 30.7 us: shards(): small_all.reshape(-1)]
    all_gather x2 -> x0, waiting for transfers between devices: 34 us -> none  [the longest x1 34 us: shards(): lax.all_gather(average_parts, 'shard', axis=0, tiled=True)]
    unnamed x1 -> x0, blocking collectives: 30.9 us -> none
    all_to_all x2 -> x0, blocking collectives: 24.9 us -> none  [the longest x1 13 us: shards(): lax.all_to_all(new_average, 'tensor', split_axis=1, concat_axis=0, tiled=...]
    add x3 -> x1, other arithmetic: 12.6 us -> 2.05 us  [shards(): valid[0] * small_grads[0].astype(jnp.float32)]
  transfers between devices with their start and end apart: 4 -> 0, of which waited for: 2 -> 0; matrix products, arithmetic and copies ran while one was open for 2% -> 0% of each run, Pallas kernels for 0% -> 0%
where the time goes in v1:
time: 154 us; the launch traced here: 153 us
  Pallas kernels  116 us (75%)
  local copies, waits for them, and re-layouts  31.1 us (20%)
  other arithmetic  3.36 us (2%)
  between operations  2.06 us (1%)
    pallas_call x1, Pallas kernels, communicate(): pl.pallas_call(step_kernel, out_shape=(rows, rows, rows, jax.ShapeDtypeSt...  105 us
    unnamed x5, local copies, waits for them, and re-layouts  26.2 us
    pallas_call x1, Pallas kernels, finish(): pl.pallas_call(finish_kernel, grid=(SHARDS // 2,), in_specs=[block, block...  11 us

profile of v1, /device:TPU:1, one launch (start us, length us, event | category | flops | bytes accessed | tf_op | source)
XLA Modules:
  0.0 152.6 jit_solution(3503038411861255861)
XLA Ops:
  2.0 0.6 pad_maximum_fusion.1.scal
  2.6 0.6 fusion.2
  3.2 2.1 %multiply_add_fusion = f32[1,368]{1,0:T(1,128)S(1)} fusion(bf16[2,368]{1,0:T(2,128)(2,1)} %param.13, f32[]{:T(128)} %bitcast.2, f32[]{:T(128)} %bitcast.1), kind=kLoop, calls=%fused_computation.5 | loop fusion | flops 1840 | bytes 2952 | tf_op jit(solution)/shard_map/add | solution.py:545
  5.3 0.7 pad_maximum_fusion
  6.0 0.4 dynamic_update_slice.7.small_in
  6.4 0.0 copy-start
  6.4 11.5 %copy.22 = bf16[2,896,2080]{2,1,0:T(8,128)(2,1)} copy(bf16[2,896,2080]{1,2,0:T(8,128)(2,1)} %param.12) | data formatting | bytes 14909440 | tf_op args[0]
  17.9 0.0 copy-done
  17.9 105.1 %step.1 = (f32[7,16640]{1,0:T(8,128)}, f32[7,16640]{1,0:T(8,128)}, f32[7,16640]{1,0:T(8,128)}, f32[8,384]{1,0:T(8,128)}, bf16[16,56,2080]{2,1,0:T(8,128)(2,1)}, /*index=5*/s16[16,56,2080]{2,1,0:T(8,128)(2,1)}) custom-call(f32[4]{0:T(128)} %pad_maximum_fusion.1.scal, f32[8,384]{1,0:T(8,128)} %copy-done, bf16[2,16,56,2080]{3,2,1,0:T(8,128)(2,1)} %bitcast.7, ...), custom_call_target="tpu_custom_call" | custom-call | tf_op jit(solution)/shard_map/step/pallas_call | solution.py:440
  122.9 1.3 fusion
  124.2 0.8 constant_dynamic-slice_fusion
  125.0 1.3 slice_reduce_fusion
  126.3 0.5 fusion.1
  126.8 11.0 %finish.1 = (bf16[16,56,2080]{2,1,0:T(8,128)(2,1)}, f32[16,56,2080]{2,1,0:T(8,128)}, f32[7,16640]{1,0:T(8,128)}, f32[7,16640]{1,0:T(8,128)}, f32[7,16640]{1,0:T(8,128)}) custom-call(bf16[16,56,2080]{2,1,0:T(8,128)(2,1)} %get-tuple-element.21.weights, s16[16,56,2080]{2,1,0:T(8,128)(2,1)} %get-tuple-element.22.codes, f32[7,16640]{1,0:T(8,128)} %get-tuple-element.23.master, ...), custom_call_target="tpu_custom_call" | custom-call | tf_op jit(solution)/shard_map/finish/pallas_call | solution.py:509
  137.8 6.2 %copy.23 = bf16[896,2080]{0,1:T(8,128)(2,1)} copy(bf16[896,2080]{1,0:T(8,128)(2,1)} %bitcast.9) | data formatting | bytes 7454720
  144.0 8.6 %copy.24 = f32[896,2080]{0,1:T(8,128)} copy(f32[896,2080]{1,0:T(8,128)} %bitcast.8) | data formatting | bytes 14909440
  (2 shorter events, 0.0 us)
Async XLA Ops:
  6.4 11.5 %copy-start = (f32[8,384]{1,0:T(8,128)}, f32[8,384]{1,0:T(8,128)S(1)}, u32[]{:S(2)}) copy-start(f32[8,384]{1,0:T(8,128)S(1)} %dynamic_update_slice.7.small_in) | copy-start | bytes 36868

commit v2 on v1

--- a/solution.py
+++ b/solution.py
@@ -1,5 +1,6 @@
 import jax
 import jax.numpy as jnp
+import numpy as np
 from jax import lax
 from jax.experimental import pallas as pl
 from jax.experimental.pallas import tpu as pltpu
@@ -48,32 +49,54 @@
     return param - learn_rate * (ratio + decay * param), first_new, second_new
 
 
+def bias(time, beta):
+    total = jnp.float32(0.0)
+    for bit in range(10):
+        term = ((time >> bit) & 1).astype(jnp.float32) * (1.0 - float(np.float32(beta)) ** (1 << bit))
+        total = total + term - total * term
+    return total
+
+
+def place(s, shape, along):
+    own = lax.broadcasted_iota(jnp.int32, shape, along)
+    every = lax.broadcasted_iota(jnp.int32, shape, 1 - along)
+    return jnp.where(jnp.logical_and(every == own + SEG * s, own < SEG), 1.0, 0.0)
+
+
+def exact_dot(a, b):
+    return jnp.dot(a, b, precision=lax.Precision.HIGHEST, preferred_element_type=jnp.float32)
+
+
 def wrap(position, shift, size):
     return lax.rem(position + (shift + size), size)
 
 
 def step_kernel(
-    scal,
-    small_in,
+    counts,
+    step,
+    small_grads,
+    small_master,
+    small_one,
+    small_two,
+    small_average,
     grads_hbm,
     master_hbm,
     one_hbm,
     two_hbm,
     average_hbm,
-    master_out,
-    one_out,
-    two_out,
+    om,
+    o1,
+    o2,
     small_out,
-    weights_out,
-    codes_out,
+    mine_out,
+    wall,
+    aall,
     gv,
+    loc,
     pm,
     p1,
     p2,
     pa,
-    om,
-    o1,
-    o2,
     big_send,
     big_recv,
     kept,
@@ -90,13 +113,12 @@
     norm_t,
     norm_y,
     norm_z,
+    small_state,
+    small_in,
     small_send,
     small_y,
     small_z,
-    wall,
-    aall,
     load_sem,
-    store_sem,
     rs_send_sem,
     rs_recv_sem,
     t_send_sem,
@@ -118,12 +140,22 @@
         return p * RING + k if axis == 0 else k * RING + p
 
     loads = []
-    for i, (src, dst) in enumerate(
-        ((grads_hbm, gv), (master_hbm, pm), (one_hbm, p1), (two_hbm, p2), (average_hbm, pa))
-    ):
-        load = pltpu.make_async_copy(src, dst, load_sem.at[i])
+    for first, width in PARTS:
+        cut = (slice(None), pl.ds(first, width))
+        loads.append((grads_hbm.at[cut], gv.at[cut]))
+    loads += [(master_hbm, pm), (one_hbm, p1), (two_hbm, p2), (average_hbm, pa)]
+    loads = [pltpu.make_async_copy(src, dst, load_sem.at[i]) for i, (src, dst) in enumerate(loads)]
+    for load in loads:
         load.start()
-        loads.append(load)
+
+    valid_one = jnp.minimum(jnp.maximum(counts[0], 0), 1).astype(jnp.float32)
+    valid_two = jnp.minimum(jnp.maximum(counts[0] - 1, 0), 1).astype(jnp.float32)
+    small_state[...] = jnp.zeros((8, 128), jnp.float32)
+    for i, ref in enumerate((small_master, small_one, small_two, small_average)):
+        small_state[pl.ds(i + 1, 1), pl.ds(0, SEG)] = ref[...]
+    small_in[...] = exact_dot(small_state[...], place(s, (128, LANES), 0))
+    micro = small_grads[...].astype(jnp.float32)
+    small_in[0:1, pl.ds(0, SMALL)] = valid_one * micro[0:1] + valid_two * micro[1:2]
 
     barrier = pltpu.get_barrier_semaphore()
     for axis in range(2):
@@ -158,24 +190,37 @@
         ]
 
     small_copies = ring_share(0, 0, small_in, small_y)
-    loads[0].wait()
-    valid_one, valid_two = scal[0], scal[1]
+
+    def turn(q, tile):
+        first, width = PARTS[q]
+        cut = pl.ds(pl.multiple_of(tile * 128, 128), 128)
+        a = gv[0, pl.ds(first, width), cut].astype(jnp.float32)
+        b = gv[1, pl.ds(first, width), cut].astype(jnp.float32)
+        loc[q][cut, :] = (valid_one * a + valid_two * b).T
 
     def local(shard, q):
-        first, width = PARTS[q]
-        a = gv[0, shard, :, pl.ds(first, width)].astype(jnp.float32)
-        b = gv[1, shard, :, pl.ds(first, width)].astype(jnp.float32)
-        return valid_one * a + valid_two * b
+        return loc[q][pl.ds(pl.multiple_of(shard * ROWS, 8), ROWS), :]
 
     axes = ((0, 1), (0, 1), (1, 0), (1, 0))
     signs = (core_sign, -core_sign, core_sign, -core_sign)
     order = [[wrap(pos[axes[q][1]], k, RING) for k in (2, signs[q], -signs[q], 0)] for q in range(4)]
     early = [[None] * 2 for _ in range(4)]
+    far = lax.min(lax.div(7 * wrap(pos[0], 2, RING), 4), 4)
     for slot in range(2):
         for q in range(4):
             axis, sign = axes[q][0], signs[q]
             p = pos[axis]
             dest = wrap(p, 2, RING) if slot == 0 else wrap(p, sign, RING)
+            if slot == 0:
+                loads[q].wait()
+            some = (0, 7) if axis == 1 else (0, 3) if slot == 0 else (3, 7)
+
+            def tile(j, carry, q=q, axis=axis):
+                turn(q, wrap(far, j, 7) if axis == 0 else j)
+                return carry
+
+            if slot == 0 or axis == 0:
+                lax.fori_loop(*some, tile, 0)
 
             def fill(k, carry, q=q, axis=axis, dest=dest, slot=slot):
                 big_send[q][slot, k] = encode(local(shard_of(axis, dest, k), q), SUM_MAX)
@@ -302,8 +347,8 @@
     norm = jnp.sqrt(norm_send[2] + norm_z[0] + norm_z[1] + norm_z[2])
     factor = jnp.minimum(1.0, clip_norm / (norm + 1e-06))[0:1, 0:1]
 
-    bias_one, bias_two = scal[2], scal[3]
-    for load in loads[1:]:
+    bias_one, bias_two = bias(step[0], beta_one), bias(step[0], beta_two)
+    for load in loads[4:]:
         load.wait()
     for copy in chunk_copies:
         copy.wait_recv()
@@ -323,11 +368,6 @@
     achunk_recv[t] = achunk_send[t]
     wchunk_copies = exchange(2, wchunk_send, wchunk_recv)
     achunk_copies = exchange(3, achunk_send, achunk_recv)
-    stores = []
-    for i, (src, dst) in enumerate(((om, master_out), (o1, one_out), (o2, two_out))):
-        store = pltpu.make_async_copy(src, dst, store_sem.at[i])
-        store.start()
-        stores.append(store)
 
     new, one, two = adam(
         small_all[1:2], small_all[2:3], small_all[3:4], small_sum * factor, bias_one, bias_two, 0.0
@@ -338,6 +378,7 @@
     small_out[2:3] = two
     small_out[3:4] = smooth
     small_out[4:8] = jnp.zeros((4, LANES), jnp.float32)
+    mine_out[...] = exact_dot(small_out[...], place(s, (LANES, 128), 1))
 
     for copy in wchunk_copies:
         copy.wait_recv()
@@ -420,38 +461,32 @@
         for j, shift in enumerate((0, -sign, sign, 2)):
             gather_wait(x, q, source(q, shift, sign), 4 + 3 * j)
             gather_wait(x, q, source(q, shift, 2), 5 + 3 * j)
-    for i, (src, dst) in enumerate(((wall, weights_out), (aall, codes_out))):
-        store = pltpu.make_async_copy(src, dst, store_sem.at[3 + i])
-        store.start()
-        stores.append(store)
     for copy in pending:
         copy.wait_send()
-    for store in stores:
-        store.wait()
-
-
-def communicate(scal, small_in, grads, master, one, two, average):
+
+
+def communicate(*args):
     hbm = pl.BlockSpec(memory_space=pl.ANY)
     vmem = pl.BlockSpec(memory_space=pltpu.VMEM)
+    smem = pl.BlockSpec(memory_space=pltpu.SMEM)
     f32, bf16, i16 = jnp.float32, jnp.bfloat16, jnp.int16
-    rows = jax.ShapeDtypeStruct((MINE, ALL_COLS), f32)
     widths = [w for _, w in PARTS]
     chunk = (TENSORS, MINE, COLS)
     return pl.pallas_call(
         step_kernel,
         out_shape=(
-            rows,
-            rows,
-            rows,
-            jax.ShapeDtypeStruct((8, LANES), f32),
-            jax.ShapeDtypeStruct((SHARDS, ROWS, COLS), bf16),
-            jax.ShapeDtypeStruct((SHARDS, ROWS, COLS), i16),
+            *[pltpu.VMEM((MINE, ALL_COLS), f32)] * 3,
+            pltpu.VMEM((8, LANES), f32),
+            pltpu.VMEM((8, 128), f32),
+            pltpu.VMEM((SHARDS, ROWS, COLS), bf16),
+            pltpu.VMEM((SHARDS, ROWS, COLS), i16),
         ),
-        in_specs=[pl.BlockSpec(memory_space=pltpu.SMEM), vmem] + [hbm] * 5,
-        out_specs=(hbm, hbm, hbm, vmem, hbm, hbm),
+        in_specs=[smem] * 2 + [vmem] * 5 + [hbm] * 5,
+        out_specs=(vmem,) * 7,
         scratch_shapes=[
-            pltpu.VMEM((2, SHARDS, ROWS, COLS), bf16),
-            *[pltpu.VMEM((MINE, ALL_COLS), f32)] * 7,
+            pltpu.VMEM((2, COLS, SHARDS * ROWS), bf16),
+            [pltpu.VMEM((SHARDS * ROWS, w), f32) for w in widths],
+            *[pltpu.VMEM((MINE, ALL_COLS), f32)] * 4,
             [pltpu.VMEM((3, RING, ROWS, w), i16) for w in widths],
             [pltpu.VMEM((3, RING, ROWS, w), i16) for w in widths],
             [pltpu.VMEM((2, ROWS, w), f32) for w in widths],
@@ -468,13 +503,12 @@
             pltpu.VMEM((TENSORS - 1, 8, 128), f32),
             pltpu.VMEM((RING - 1, 8, 128), f32),
             pltpu.VMEM((RING - 1, 8, 128), f32),
+            pltpu.VMEM((8, 128), f32),
+            pltpu.VMEM((8, LANES), f32),
             pltpu.VMEM((8, LANES), f32),
             pltpu.VMEM((RING - 1, 8, LANES), f32),
             pltpu.VMEM((RING - 1, 8, LANES), f32),
-            pltpu.VMEM((SHARDS, ROWS, COLS), bf16),
-            pltpu.VMEM((SHARDS, ROWS, COLS), i16),
-            pltpu.SemaphoreType.DMA((5,)),
-            pltpu.SemaphoreType.DMA((5,)),
+            pltpu.SemaphoreType.DMA((8,)),
             pltpu.SemaphoreType.DMA((4, 9)),
             pltpu.SemaphoreType.DMA((4, 9)),
             pltpu.SemaphoreType.DMA((4, TENSORS)),
@@ -485,41 +519,92 @@
             pltpu.SemaphoreType.DMA((2, 4, 15)),
         ],
         compiler_params=pltpu.CompilerParams(
-            collective_id=0, has_side_effects=True, vmem_limit_bytes=60 * 1024 * 1024
+            collective_id=0, has_side_effects=True, vmem_limit_bytes=48 * 1024 * 1024
         ),
         name="step",
-    )(scal, small_in, grads, master, one, two, average)
-
-
-def finish_kernel(weights, codes, master, one, two, weights_out, average_out, master_out, one_out, two_out):
-    weights_out[...] = weights[...]
-    average_out[...] = decode(codes[...], AVERAGE_MAX)
-
-    @pl.when(pl.program_id(0) == 0)
+    )(*args)
+
+
+TURN = 256
+
+
+def finish_kernel(
+    weights,
+    codes,
+    master,
+    one,
+    two,
+    small,
+    mine,
+    weights_out,
+    average_out,
+    master_out,
+    one_out,
+    two_out,
+    small_out,
+    small_one_out,
+    small_two_out,
+    small_weights_out,
+    small_average_out,
+):
+    step = pl.program_id(0)
+    last = COLS // TURN
+
+    def turn(width, first):
+        cut = (slice(None), slice(None), pl.ds(first, width))
+        weights_out[pl.ds(0, width), :] = weights[cut].reshape(SHARDS * ROWS, width).T
+        code = codes[cut].astype(jnp.int32).reshape(SHARDS * ROWS, width).T
+        average_out[pl.ds(0, width), :] = decode(code, AVERAGE_MAX)
+
+    @pl.when(step < last)
+    def _():
+        turn(TURN, pl.multiple_of(step * TURN, TURN))
+
+    @pl.when(step == last)
+    def _():
+        turn(COLS - last * TURN, last * TURN)
+
+    @pl.when(step == 0)
     def _():
         master_out[...] = master[...]
         one_out[...] = one[...]
         two_out[...] = two[...]
-
-
-def finish(weights, codes, master, one, two):
-    block = pl.BlockSpec((2, ROWS, COLS), lambda i: (i, 0, 0))
-    whole = pl.BlockSpec((MINE, ALL_COLS), lambda i: (0, 0))
-    rows = jax.ShapeDtypeStruct((MINE, ALL_COLS), jnp.float32)
+        small_out[...] = mine[0:1, 0:SEG]
+        small_one_out[...] = mine[1:2, 0:SEG]
+        small_two_out[...] = mine[2:3, 0:SEG]
+        small_weights_out[...] = small[0:1, 0:SMALL].astype(jnp.bfloat16)
+        small_average_out[...] = small[3:4, 0:SMALL]
+
+
+def finish(weights, codes, master, one, two, small, mine):
+    def whole(*shape):
+        return pl.BlockSpec(shape, lambda i: (0,) * len(shape))
+
+    vmem = pl.BlockSpec(memory_space=pltpu.VMEM)
+    f32, bf16 = jnp.float32, jnp.bfloat16
+    rows = jax.ShapeDtypeStruct((MINE, ALL_COLS), f32)
+    few = jax.ShapeDtypeStruct((1, SEG), f32)
+    turned = pl.BlockSpec((TURN, SHARDS * ROWS), lambda i: (i, 0))
     return pl.pallas_call(
         finish_kernel,
-        grid=(SHARDS // 2,),
-        in_specs=[block, block, whole, whole, whole],
-        out_specs=[block, block, whole, whole, whole],
+        grid=(pl.cdiv(COLS, TURN),),
+        in_specs=[vmem] * 7,
+        out_specs=[turned, turned] + [whole(MINE, ALL_COLS)] * 3 + [whole(1, SEG)] * 3 + [whole(1, SMALL)] * 2,
         out_shape=(
-            jax.ShapeDtypeStruct((SHARDS, ROWS, COLS), jnp.bfloat16),
-            jax.ShapeDtypeStruct((SHARDS, ROWS, COLS), jnp.float32),
+            jax.ShapeDtypeStruct((COLS, SHARDS * ROWS), bf16),
+            jax.ShapeDtypeStruct((COLS, SHARDS * ROWS), f32),
             rows,
             rows,
             rows,
+            few,
+            few,
+            few,
+            jax.ShapeDtypeStruct((1, SMALL), bf16),
+            jax.ShapeDtypeStruct((1, SMALL), f32),
         ),
+        compiler_params=pltpu.CompilerParams(vmem_limit_bytes=32 * 1024 * 1024),
         name="finish",
-    )(weights, codes, master, one, two)
+    )(weights, codes, master, one, two, small, mine)
 
 
 def shards(
@@ -536,33 +621,34 @@
     small_two,
     small_average,
 ):
-    s = lax.axis_index("shard")
-    valid = (jnp.arange(2, dtype=jnp.int32) < counts[0]).astype(jnp.float32)
-    time = step[0].astype(jnp.float32)
-    bias_one = 1.0 - jnp.power(jnp.float32(beta_one), time)
-    bias_two = 1.0 - jnp.power(jnp.float32(beta_two), time)
-    scal = jnp.stack([valid[0], valid[1], bias_one, bias_two])
-    small_term = valid[0] * small_grads[0].astype(jnp.float32) + valid[1] * small_grads[1].astype(jnp.float32)
-    state = jnp.concatenate([small_master, small_one, small_two, small_average], axis=0)
-    small_in = jnp.zeros((8, LANES), jnp.float32)
-    small_in = lax.dynamic_update_slice(small_in, small_term[None], (0, 0))
-    small_in = lax.dynamic_update_slice(small_in, state, (1, SEG * s))
-    new_master, new_one, new_two, small_new, weights, codes = communicate(
-        scal, small_in, grads.reshape(2, SHARDS, ROWS, COLS), master, moment_one, moment_two, average
+    new_master, new_one, new_two, small, mine, weights, codes = communicate(
+        counts,
+        step,
+        small_grads,
+        small_master,
+        small_one,
+        small_two,
+        small_average,
+        grads.transpose(0, 2, 1),
+        master,
+        moment_one,
+        moment_two,
+        average,
     )
-    weights, averages, new_master, new_one, new_two = finish(weights, codes, new_master, new_one, new_two)
-    mine = lax.dynamic_slice(small_new, (0, SEG * s), (3, SEG))
+    (weights, averages, new_master, new_one, new_two, small_new, small_new_one, small_new_two, small_weights, small_averages) = finish(
+        weights, codes, new_master, new_one, new_two, small, mine
+    )
     return (
         new_master,
         new_one,
         new_two,
-        mine[0:1],
-        mine[1:2],
-        mine[2:3],
-        weights.reshape(SHARDS * ROWS, COLS),
-        small_new[0, :SMALL].astype(jnp.bfloat16),
-        averages.reshape(SHARDS * ROWS, COLS),
-        small_new[3, :SMALL],
+        small_new,
+        small_new_one,
+        small_new_two,
+        weights.T,
+        small_weights.reshape(SMALL),
+        averages.T,
+        small_averages.reshape(SMALL),
     )
 
 

time: 154 us -> 113 us (0.73)
  local copies, waits for them, and re-layouts: 31.1 us -> 0 us
  Pallas kernels: 116 us -> 110 us
  other arithmetic: 3.36 us -> 1.18 us
    unnamed x5 -> x0, local copies, waits for them, and re-layouts: 26.2 us -> none
    pallas_call x2, Pallas kernels: 116 us -> 110 us  [the longest x1 102 us: communicate(): pl.pallas_call(step_kernel, out_shape=(*[pltpu.VMEM((MINE, ALL_COLS), f32...]
    slice x4 -> x0, local copies, waits for them, and re-layouts: 3.69 us -> none  [the longest x1 1.3 us: shards(): small_new[3, :SMALL]]
    add x1 -> x0, other arithmetic: 2.05 us -> none  [shards(): valid[0] * small_grads[0].astype(jnp.float32)]
where the time goes in v2:
time: 113 us
  Pallas kernels  110 us (97%)
  between operations  1.95 us (2%)
  other arithmetic  1.18 us (1%)
    pallas_call x1, Pallas kernels, communicate(): pl.pallas_call(step_kernel, out_shape=(*[pltpu.VMEM((MINE, ALL_COLS), f32...  102 us
    pallas_call x1, Pallas kernels, finish(): pl.pallas_call(finish_kernel, grid=(pl.cdiv(COLS, TURN),), in_specs=[vmem...  7.63 us

profile of v2, /device:TPU:1, one launch (start us, length us, event | category | flops | bytes accessed | tf_op | source)
XLA Modules:
  0.0 113.0 jit_solution(4253741326169995139)
XLA Ops:
  1.9 102.3 %step.2 = (f32[7,16640]{1,0:T(8,128)S(1)}, f32[7,16640]{1,0:T(8,128)S(1)}, f32[7,16640]{1,0:T(8,128)S(1)}, f32[8,384]{1,0:T(8,128)S(1)}, f32[8,128]{1,0:T(8,128)...) custom-call(s32[1]{0:T(128)S(6)} %copy.22.counts, s32[1]{0:T(128)S(6)} %copy.23.step, ...), custom_call_target="tpu_custom_call" | custom-call | tf_op jit(solution)/shard_map/step/pallas_call | solution.py:475
  104.2 7.6 %finish.1 = (bf16[2080,896]{1,0:T(8,128)(2,1)}, f32[2080,896]{1,0:T(8,128)}, f32[7,16640]{1,0:T(8,128)}, f32[7,16640]{1,0:T(8,128)}, f32[7,16640]{1,0:T(8,128)},...) custom-call(bf16[16,56,2080]{2,1,0:T(8,128)(2,1)S(1)} %get-tuple-ele, ...), custom_call_target="tpu_custom_call" | custom-call | tf_op jit(solution)/shard_map/finish/pallas_call | solution.py:588
  111.9 0.6 reduce
  112.4 0.6 reduce.1

commit v3 on v2

--- a/solution.py
+++ b/solution.py
@@ -28,7 +28,8 @@
 PARTS = ((0, 512), (512, 512), (1024, 512), (1536, 544))
 TOP = 32700.0
 SUM_MAX = 2.0
-AVERAGE_MAX = 0.03
+AVERAGE_MAX = 0.02
+WEIGHT_UNIT = 2.0**-33
 
 
 def encode(x, most):
@@ -40,6 +41,26 @@
 def decode(code, most):
     root = code.astype(jnp.int32).astype(jnp.float32)
     return (root * root) * (root * jnp.abs(root)) * (most / TOP**4)
+
+
+def encode_weight(x):
+    units = jnp.minimum(jnp.abs(x) * (1.0 / WEIGHT_UNIT), 2147483520.0)
+    whole = units.astype(jnp.int32)
+    shift = jnp.zeros_like(whole)
+    for bits in (16, 8, 4, 2, 1):
+        shift = shift + jnp.where((whole >> shift) >= (1 << (bits + 10)), bits, 0)
+    kept = whole >> shift
+    cut = jnp.logical_or((kept << shift) != whole, whole.astype(jnp.float32) != units)
+    code = ((shift << 10) + kept) | jnp.where(cut, 1, 0)
+    return jnp.where(x < 0.0, -code, code).astype(jnp.int16)
+
+
+def decode_weight(code):
+    code = code.astype(jnp.int32)
+    size = jnp.abs(code)
+    shift = jnp.maximum((size >> 10) - 1, 0)
+    value = ((size - (shift << 10)) << shift).astype(jnp.float32)
+    return jnp.where(code < 0, -WEIGHT_UNIT, WEIGHT_UNIT) * value
 
 
 def adam(param, first, second, gradient, bias_one, bias_two, decay):
@@ -90,7 +111,7 @@
     small_out,
     mine_out,
     wall,
-    aall,
+    smooth_out,
     gv,
     loc,
     pm,
@@ -109,6 +130,7 @@
     wchunk_recv,
     achunk_send,
     achunk_recv,
+    aall,
     norm_send,
     norm_t,
     norm_y,
@@ -139,11 +161,11 @@
     def shard_of(axis, p, k):
         return p * RING + k if axis == 0 else k * RING + p
 
-    loads = []
+    loads = [(average_hbm, pa)]
     for first, width in PARTS:
         cut = (slice(None), pl.ds(first, width))
         loads.append((grads_hbm.at[cut], gv.at[cut]))
-    loads += [(master_hbm, pm), (one_hbm, p1), (two_hbm, p2), (average_hbm, pa)]
+    loads += [(master_hbm, pm), (one_hbm, p1), (two_hbm, p2)]
     loads = [pltpu.make_async_copy(src, dst, load_sem.at[i]) for i, (src, dst) in enumerate(loads)]
     for load in loads:
         load.start()
@@ -189,6 +211,24 @@
             for d in range(1, RING)
         ]
 
+    def exchange(kind, src, dst):
+        copies = []
+        for d in range(1, TENSORS):
+            to = wrap(t, d, TENSORS)
+            copies.append(
+                send(src.at[to], dst.at[t], t_send_sem.at[kind, d], t_recv_sem.at[kind, d], (s, to))
+            )
+        return copies
+
+    loads[0].wait()
+    half = ALL_COLS // 2
+    for h in range(2):
+        codes = pa[:, pl.ds(half * h, half)]
+        for j in range(4):
+            achunk_send[4 * h + j] = encode(codes[:, COLS * j : COLS * (j + 1)], AVERAGE_MAX)
+    achunk_recv[t] = achunk_send[t]
+    achunk_copies = exchange(3, achunk_send, achunk_recv)
+
     small_copies = ring_share(0, 0, small_in, small_y)
 
     def turn(q, tile):
@@ -204,6 +244,90 @@
     axes = ((0, 1), (0, 1), (1, 0), (1, 0))
     signs = (core_sign, -core_sign, core_sign, -core_sign)
     order = [[wrap(pos[axes[q][1]], k, RING) for k in (2, signs[q], -signs[q], 0)] for q in range(4)]
+    arrays = (wall, aall)
+
+    def gather_send(x, q, shard, index, axis, sign):
+        first, width = PARTS[q]
+        ref = arrays[x].at[shard, :, pl.ds(first, width)]
+        send(
+            ref,
+            ref,
+            ag_send_sem.at[x, q, index],
+            ag_recv_sem.at[x, q, index],
+            ring_device(axis, wrap(pos[axis], sign, RING)),
+        )
+
+    def gather_wait(x, q, shard, index):
+        first, width = PARTS[q]
+        ref = arrays[x].at[shard, :, pl.ds(first, width)]
+        pltpu.make_async_remote_copy(
+            src_ref=ref,
+            dst_ref=ref,
+            send_sem=ag_send_sem.at[x, q, index],
+            recv_sem=ag_recv_sem.at[x, q, index],
+            device_id=ring_device(0, wrap(pos[0], 1, RING)),
+            device_id_type=MESH,
+        ).wait_recv()
+
+    def outer(x, q, j, shard):
+        axis, sign = axes[q][0], signs[q]
+        gather_send(x, q, shard, 3 + 3 * j, axis, sign)
+        gather_send(x, q, shard, 4 + 3 * j, axis, -sign)
+
+    def source(q, shift, shift_outer):
+        axis, other = axes[q]
+        return shard_of(axis, wrap(pos[axis], shift_outer, RING), wrap(pos[other], shift, RING))
+
+    def relay(x, q, j, shift):
+        axis, sign = axes[q][0], signs[q]
+        shard = source(q, shift, -sign)
+        gather_wait(x, q, shard, 3 + 3 * j)
+        gather_send(x, q, shard, 5 + 3 * j, axis, sign)
+
+    def gather_first(x, q):
+        other, sign = axes[q][1], signs[q]
+        gather_send(x, q, s, 0, other, sign)
+        gather_send(x, q, s, 1, other, -sign)
+        outer(x, q, 0, s)
+
+    def gather_second(x, q):
+        other, sign = axes[q][1], signs[q]
+        shard = source(q, -sign, 0)
+        gather_wait(x, q, shard, 0)
+        gather_send(x, q, shard, 2, other, sign)
+        outer(x, q, 1, shard)
+        relay(x, q, 0, 0)
+
+    def gather_third(x, q):
+        sign = signs[q]
+        shard = source(q, sign, 0)
+        gather_wait(x, q, shard, 1)
+        outer(x, q, 2, shard)
+        relay(x, q, 1, -sign)
+
+    def gather_fourth(x, q):
+        sign = signs[q]
+        shard = source(q, 2, 0)
+        gather_wait(x, q, shard, 2)
+        outer(x, q, 3, shard)
+        relay(x, q, 2, sign)
+
+    def gather_fifth(x, q):
+        relay(x, q, 3, 2)
+
+    def gather_end(x, q):
+        sign = signs[q]
+        for j, shift in enumerate((0, -sign, sign, 2)):
+            gather_wait(x, q, source(q, shift, sign), 4 + 3 * j)
+            gather_wait(x, q, source(q, shift, 2), 5 + 3 * j)
+
+    def turn_average(q):
+        first, width = PARTS[q]
+        for c in range(0, width, 128):
+            some = min(128, width - c)
+            codes = aall[:, :, pl.ds(first + c, some)].astype(jnp.int32).reshape(SHARDS * ROWS, some)
+            smooth_out[pl.ds(first + c, some), :] = decay_rate * decode(codes.T, AVERAGE_MAX)
+
     early = [[None] * 2 for _ in range(4)]
     far = lax.min(lax.div(7 * wrap(pos[0], 2, RING), 4), 4)
     for slot in range(2):
@@ -212,7 +336,7 @@
             p = pos[axis]
             dest = wrap(p, 2, RING) if slot == 0 else wrap(p, sign, RING)
             if slot == 0:
-                loads[q].wait()
+                loads[q + 1].wait()
             some = (0, 7) if axis == 1 else (0, 3) if slot == 0 else (3, 7)
 
             def tile(j, carry, q=q, axis=axis):
@@ -258,6 +382,9 @@
     small_copies = ring_share(1, 1, small_send, small_z)
     for q in range(4):
         early[q][1].wait_recv()
+    for copy in achunk_copies:
+        copy.wait_recv()
+    aall[s] = jnp.concatenate([achunk_recv[j].astype(jnp.int32) for j in range(TENSORS)], axis=0).astype(jnp.int16)
 
     later = [[None] * 3 for _ in range(4)]
     for i in range(RING):
@@ -293,6 +420,8 @@
             rs_recv_sem.at[q, 8],
             ring_device(other, wrap(pos[other], -sign, RING)),
         )
+    for q in range(4):
+        gather_first(1, q)
     for copy in small_copies:
         copy.wait_recv()
     small_all = small_send[...] + small_z[0] + small_z[1] + small_z[2]
@@ -322,15 +451,6 @@
         chunk_send[j] = encode(total[pl.ds(MINE * j, MINE), :], 16 * SUM_MAX)
     chunk_recv[t] = chunk_send[t]
 
-    def exchange(kind, src, dst):
-        copies = []
-        for d in range(1, TENSORS):
-            to = wrap(t, d, TENSORS)
-            copies.append(
-                send(src.at[to], dst.at[t], t_send_sem.at[kind, d], t_recv_sem.at[kind, d], (s, to))
-            )
-        return copies
-
     chunk_copies = exchange(1, chunk_send, chunk_recv)
     for copy in norm_copies:
         copy.wait_recv()
@@ -342,17 +462,19 @@
         copy.wait_recv()
     norm = norm_send[1] + norm_y[0] + norm_y[1] + norm_y[2]
     norm_send[2] = norm
-    for copy in ring_share(3, 1, norm_send.at[2], norm_z):
+    norm_copies = ring_share(3, 1, norm_send.at[2], norm_z)
+    for q in range(4):
+        gather_second(1, q)
+    for copy in norm_copies:
         copy.wait_recv()
     norm = jnp.sqrt(norm_send[2] + norm_z[0] + norm_z[1] + norm_z[2])
     factor = jnp.minimum(1.0, clip_norm / (norm + 1e-06))[0:1, 0:1]
 
     bias_one, bias_two = bias(step[0], beta_one), bias(step[0], beta_two)
-    for load in loads[4:]:
+    for load in loads[5:]:
         load.wait()
     for copy in chunk_copies:
         copy.wait_recv()
-    half = ALL_COLS // 2
     for h in range(2):
         cols = pl.ds(half * h, half)
         summed = jnp.concatenate([decode(chunk_recv[4 * h + j], 16 * SUM_MAX) for j in range(4)], axis=1)
@@ -360,14 +482,12 @@
         om[:, cols] = new
         o1[:, cols] = one
         o2[:, cols] = two
-        smooth = decay_rate * pa[:, cols] + (1.0 - decay_rate) * new
         for j in range(4):
-            wchunk_send[4 * h + j] = new[:, COLS * j : COLS * (j + 1)].astype(jnp.bfloat16)
-            achunk_send[4 * h + j] = encode(smooth[:, COLS * j : COLS * (j + 1)], AVERAGE_MAX)
+            wchunk_send[4 * h + j] = encode_weight(new[:, COLS * j : COLS * (j + 1)])
     wchunk_recv[t] = wchunk_send[t]
-    achunk_recv[t] = achunk_send[t]
     wchunk_copies = exchange(2, wchunk_send, wchunk_recv)
-    achunk_copies = exchange(3, achunk_send, achunk_recv)
+    for q in range(4):
+        gather_third(1, q)
 
     new, one, two = adam(
         small_all[1:2], small_all[2:3], small_all[3:4], small_sum * factor, bias_one, bias_two, 0.0
@@ -380,87 +500,31 @@
     small_out[4:8] = jnp.zeros((4, LANES), jnp.float32)
     mine_out[...] = exact_dot(small_out[...], place(s, (LANES, 128), 1))
 
+    for q in range(4):
+        gather_fourth(1, q)
     for copy in wchunk_copies:
         copy.wait_recv()
-    rows = jnp.concatenate([wchunk_recv[j].astype(jnp.float32) for j in range(TENSORS)], axis=0)
-    wall[s] = rows.astype(jnp.bfloat16)
-    for copy in achunk_copies:
-        copy.wait_recv()
-    rows = jnp.concatenate([achunk_recv[j].astype(jnp.int32) for j in range(TENSORS)], axis=0)
-    aall[s] = rows.astype(jnp.int16)
-
-    arrays = (wall, aall)
-    lanes = [(x, q) for x in range(2) for q in range(4)]
-
-    def gather_send(x, q, shard, index, axis, sign):
-        first, width = PARTS[q]
-        ref = arrays[x].at[shard, :, pl.ds(first, width)]
-        send(
-            ref,
-            ref,
-            ag_send_sem.at[x, q, index],
-            ag_recv_sem.at[x, q, index],
-            ring_device(axis, wrap(pos[axis], sign, RING)),
-        )
-
-    def gather_wait(x, q, shard, index):
-        first, width = PARTS[q]
-        ref = arrays[x].at[shard, :, pl.ds(first, width)]
-        pltpu.make_async_remote_copy(
-            src_ref=ref,
-            dst_ref=ref,
-            send_sem=ag_send_sem.at[x, q, index],
-            recv_sem=ag_recv_sem.at[x, q, index],
-            device_id=ring_device(0, wrap(pos[0], 1, RING)),
-            device_id_type=MESH,
-        ).wait_recv()
-
-    def outer(x, q, j, shard):
-        axis, sign = axes[q][0], signs[q]
-        gather_send(x, q, shard, 3 + 3 * j, axis, sign)
-        gather_send(x, q, shard, 4 + 3 * j, axis, -sign)
-
-    def source(q, shift, shift_outer):
-        axis, other = axes[q]
-        return shard_of(axis, wrap(pos[axis], shift_outer, RING), wrap(pos[other], shift, RING))
-
-    def relay(x, q, j, shift):
-        axis, sign = axes[q][0], signs[q]
-        shard = source(q, shift, -sign)
-        gather_wait(x, q, shard, 3 + 3 * j)
-        gather_send(x, q, shard, 5 + 3 * j, axis, sign)
-
-    for x, q in lanes:
-        other, sign = axes[q][1], signs[q]
-        gather_send(x, q, s, 0, other, sign)
-        gather_send(x, q, s, 1, other, -sign)
-        outer(x, q, 0, s)
-    for x, q in lanes:
-        other, sign = axes[q][1], signs[q]
-        shard = source(q, -sign, 0)
-        gather_wait(x, q, shard, 0)
-        gather_send(x, q, shard, 2, other, sign)
-        outer(x, q, 1, shard)
-        relay(x, q, 0, 0)
-    for x, q in lanes:
-        sign = signs[q]
-        shard = source(q, sign, 0)
-        gather_wait(x, q, shard, 1)
-        outer(x, q, 2, shard)
-        relay(x, q, 1, -sign)
-    for x, q in lanes:
-        sign = signs[q]
-        shard = source(q, 2, 0)
-        gather_wait(x, q, shard, 2)
-        outer(x, q, 3, shard)
-        relay(x, q, 2, sign)
-    for x, q in lanes:
-        relay(x, q, 3, 2)
-    for x, q in lanes:
-        sign = signs[q]
-        for j, shift in enumerate((0, -sign, sign, 2)):
-            gather_wait(x, q, source(q, shift, sign), 4 + 3 * j)
-            gather_wait(x, q, source(q, shift, 2), 5 + 3 * j)
+    wall[s] = jnp.concatenate([wchunk_recv[j].astype(jnp.int32) for j in range(TENSORS)], axis=0).astype(jnp.int16)
+    for q in range(4):
+        gather_first(0, q)
+    for q in range(4):
+        gather_fifth(1, q)
+    for q in range(4):
+        gather_second(0, q)
+    for q in range(4):
+        gather_end(1, q)
+    turn_average(0)
+    for q in range(4):
+        gather_third(0, q)
+    turn_average(1)
+    for q in range(4):
+        gather_fourth(0, q)
+    turn_average(2)
+    for q in range(4):
+        gather_fifth(0, q)
+    turn_average(3)
+    for q in range(4):
+        gather_end(0, q)
     for copy in pending:
         copy.wait_send()
 
@@ -478,8 +542,8 @@
             *[pltpu.VMEM((MINE, ALL_COLS), f32)] * 3,
             pltpu.VMEM((8, LANES), f32),
             pltpu.VMEM((8, 128), f32),
-            pltpu.VMEM((SHARDS, ROWS, COLS), bf16),
             pltpu.VMEM((SHARDS, ROWS, COLS), i16),
+            pltpu.VMEM((COLS, SHARDS * ROWS), f32),
         ),
         in_specs=[smem] * 2 + [vmem] * 5 + [hbm] * 5,
         out_specs=(vmem,) * 7,
@@ -495,10 +559,11 @@
             pltpu.VMEM((ROWS, COLS), f32),
             pltpu.VMEM(chunk, i16),
             pltpu.VMEM(chunk, i16),
-            pltpu.VMEM(chunk, bf16),
-            pltpu.VMEM(chunk, bf16),
             pltpu.VMEM(chunk, i16),
             pltpu.VMEM(chunk, i16),
+            pltpu.VMEM(chunk, i16),
+            pltpu.VMEM(chunk, i16),
+            pltpu.VMEM((SHARDS, ROWS, COLS), i16),
             pltpu.VMEM((3, 8, 128), f32),
             pltpu.VMEM((TENSORS - 1, 8, 128), f32),
             pltpu.VMEM((RING - 1, 8, 128), f32),
@@ -529,8 +594,8 @@
 
 
 def finish_kernel(
-    weights,
     codes,
+    smooth,
     master,
     one,
     two,
@@ -552,9 +617,9 @@
 
     def turn(width, first):
         cut = (slice(None), slice(None), pl.ds(first, width))
-        weights_out[pl.ds(0, width), :] = weights[cut].reshape(SHARDS * ROWS, width).T
-        code = codes[cut].astype(jnp.int32).reshape(SHARDS * ROWS, width).T
-        average_out[pl.ds(0, width), :] = decode(code, AVERAGE_MAX)
+        new = decode_weight(codes[cut].astype(jnp.int32).reshape(SHARDS * ROWS, width).T)
+        weights_out[pl.ds(0, width), :] = new.astype(jnp.bfloat16)
+        average_out[pl.ds(0, width), :] = smooth[pl.ds(first, width), :] + (1.0 - decay_rate) * new
 
     @pl.when(step < last)
     def _():
@@ -576,7 +641,7 @@
         small_average_out[...] = small[3:4, 0:SMALL]
 
 
-def finish(weights, codes, master, one, two, small, mine):
+def finish(codes, smooth, master, one, two, small, mine):
     def whole(*shape):
         return pl.BlockSpec(shape, lambda i: (0,) * len(shape))
 
@@ -604,7 +669,7 @@
         ),
         compiler_params=pltpu.CompilerParams(vmem_limit_bytes=32 * 1024 * 1024),
         name="finish",
-    )(weights, codes, master, one, two, small, mine)
+    )(codes, smooth, master, one, two, small, mine)
 
 
 def shards(
@@ -621,7 +686,7 @@
     small_two,
     small_average,
 ):
-    new_master, new_one, new_two, small, mine, weights, codes = communicate(
+    new_master, new_one, new_two, small, mine, codes, smooth = communicate(
         counts,
         step,
         small_grads,
@@ -636,7 +701,7 @@
         average,
     )
     (weights, averages, new_master, new_one, new_two, small_new, small_new_one, small_new_two, small_weights, small_averages) = finish(
-        weights, codes, new_master, new_one, new_two, small, mine
+        codes, smooth, new_master, new_one, new_two, small, mine
     )
     return (
         new_master,

time: 113 us -> 96.7 us (0.86)
  Pallas kernels: 110 us -> 92.6 us
    pallas_call x1, Pallas kernels: 102 us -> 84.5 us  [communicate(): pl.pallas_call(step_kernel, out_shape=(*[pltpu.VMEM((MINE, ALL_COLS), f32...]
where the time goes in v3:
time: 96.7 us; the launch traced here: 95.7 us
  Pallas kernels  92.6 us (96%)
  between operations  1.95 us (2%)
  other arithmetic  1.18 us (1%)
    pallas_call x1, Pallas kernels, communicate(): pl.pallas_call(step_kernel, out_shape=(*[pltpu.VMEM((MINE, ALL_COLS), f32...  84.5 us
    pallas_call x1, Pallas kernels, finish(): pl.pallas_call(finish_kernel, grid=(pl.cdiv(COLS, TURN),), in_specs=[vmem...  8.1 us

profile of v3, /device:TPU:1, one launch (start us, length us, event | category | flops | bytes accessed | tf_op | source)
XLA Modules:
  0.0 95.7 jit_solution(178336084808441522)
XLA Ops:
  1.9 84.5 %step.2 = (f32[7,16640]{1,0:T(8,128)S(1)}, f32[7,16640]{1,0:T(8,128)S(1)}, f32[7,16640]{1,0:T(8,128)S(1)}, f32[8,384]{1,0:T(8,128)S(1)}, f32[8,128]{1,0:T(8,128)...) custom-call(s32[1]{0:T(128)S(6)} %copy.22.counts, s32[1]{0:T(128)S(6)} %copy.23.step, ...), custom_call_target="tpu_custom_call" | custom-call | tf_op jit(solution)/shard_map/step/pallas_call | solution.py:539
  86.4 8.1 %finish.1 = (bf16[2080,896]{1,0:T(8,128)(2,1)}, f32[2080,896]{1,0:T(8,128)}, f32[7,16640]{1,0:T(8,128)}, f32[7,16640]{1,0:T(8,128)}, f32[7,16640]{1,0:T(8,128)},...) custom-call(s16[16,56,2080]{2,1,0:T(8,128)(2,1)S(1)} %get-tuple-elem, ...), custom_call_target="tpu_custom_call" | custom-call | tf_op jit(solution)/shard_map/finish/pallas_call | solution.py:653
  94.5 0.6 reduce
  95.1 0.6 reduce.1

commit v4 on v3

--- a/solution.py
+++ b/solution.py
@@ -25,7 +25,7 @@
 SMALL = 368
 SEG = 23
 LANES = 384
-PARTS = ((0, 512), (512, 512), (1024, 512), (1536, 544))
+PARTS = ((0, 512), (1536, 544), (512, 512), (1024, 512))
 TOP = 32700.0
 SUM_MAX = 2.0
 AVERAGE_MAX = 0.02
@@ -133,8 +133,7 @@
     aall,
     norm_send,
     norm_t,
-    norm_y,
-    norm_z,
+    norm_s,
     small_state,
     small_in,
     small_send,
@@ -145,6 +144,8 @@
     rs_recv_sem,
     t_send_sem,
     t_recv_sem,
+    n_send_sem,
+    n_recv_sem,
     r_send_sem,
     r_recv_sem,
     ag_send_sem,
@@ -180,14 +181,11 @@
     small_in[0:1, pl.ds(0, SMALL)] = valid_one * micro[0:1] + valid_two * micro[1:2]
 
     barrier = pltpu.get_barrier_semaphore()
-    for axis in range(2):
-        for d in range(1, RING):
-            pl.semaphore_signal(
-                barrier, inc=1, device_id=ring_device(axis, wrap(pos[axis], d, RING)), device_id_type=MESH
-            )
+    for d in range(1, SHARDS):
+        pl.semaphore_signal(barrier, inc=1, device_id=(wrap(s, d, SHARDS), t), device_id_type=MESH)
     for d in range(1, TENSORS):
         pl.semaphore_signal(barrier, inc=1, device_id=(s, wrap(t, d, TENSORS)), device_id_type=MESH)
-    pl.semaphore_wait(barrier, 2 * (RING - 1) + TENSORS - 1)
+    pl.semaphore_wait(barrier, SHARDS - 1 + TENSORS - 1)
 
     pending = []
 
@@ -297,13 +295,12 @@
         gather_send(x, q, shard, 2, other, sign)
         outer(x, q, 1, shard)
         relay(x, q, 0, 0)
-
-    def gather_third(x, q):
-        sign = signs[q]
         shard = source(q, sign, 0)
         gather_wait(x, q, shard, 1)
         outer(x, q, 2, shard)
-        relay(x, q, 1, -sign)
+
+    def gather_third(x, q):
+        relay(x, q, 1, -signs[q])
 
     def gather_fourth(x, q):
         sign = signs[q]
@@ -458,16 +455,21 @@
     for d in range(TENSORS - 1):
         norm = norm + norm_t[d]
     norm_send[1] = norm
-    for copy in ring_share(2, 0, norm_send.at[1], norm_y):
-        copy.wait_recv()
-    norm = norm_send[1] + norm_y[0] + norm_y[1] + norm_y[2]
-    norm_send[2] = norm
-    norm_copies = ring_share(3, 1, norm_send.at[2], norm_z)
+    norm_copies = []
+    for d in range(1, SHARDS):
+        to = wrap(s, d, SHARDS)
+        norm_copies.append(
+            send(norm_send.at[1], norm_s.at[s], n_send_sem.at[d], n_recv_sem.at[d], (to, t))
+        )
+    norm_s[s] = norm
     for q in range(4):
         gather_second(1, q)
     for copy in norm_copies:
         copy.wait_recv()
-    norm = jnp.sqrt(norm_send[2] + norm_z[0] + norm_z[1] + norm_z[2])
+    norm = norm_s[0]
+    for d in range(1, SHARDS):
+        norm = norm + norm_s[d]
+    norm = jnp.sqrt(norm)
     factor = jnp.minimum(1.0, clip_norm / (norm + 1e-06))[0:1, 0:1]
 
     bias_one, bias_two = bias(step[0], beta_one), bias(step[0], beta_two)
@@ -513,16 +515,14 @@
         gather_second(0, q)
     for q in range(4):
         gather_end(1, q)
-    turn_average(0)
     for q in range(4):
         gather_third(0, q)
-    turn_average(1)
     for q in range(4):
         gather_fourth(0, q)
-    turn_average(2)
     for q in range(4):
         gather_fifth(0, q)
-    turn_average(3)
+    for i in range(4):
+        turn_average(i)
     for q in range(4):
         gather_end(0, q)
     for copy in pending:
@@ -564,10 +564,9 @@
             pltpu.VMEM(chunk, i16),
             pltpu.VMEM(chunk, i16),
             pltpu.VMEM((SHARDS, ROWS, COLS), i16),
-            pltpu.VMEM((3, 8, 128), f32),
+            pltpu.VMEM((2, 8, 128), f32),
             pltpu.VMEM((TENSORS - 1, 8, 128), f32),
-            pltpu.VMEM((RING - 1, 8, 128), f32),
-            pltpu.VMEM((RING - 1, 8, 128), f32),
+            pltpu.VMEM((SHARDS, 8, 128), f32),
             pltpu.VMEM((8, 128), f32),
             pltpu.VMEM((8, LANES), f32),
             pltpu.VMEM((8, LANES), f32),
@@ -578,8 +577,10 @@
             pltpu.SemaphoreType.DMA((4, 9)),
             pltpu.SemaphoreType.DMA((4, TENSORS)),
             pltpu.SemaphoreType.DMA((4, TENSORS)),
-            pltpu.SemaphoreType.DMA((4, RING - 1)),
-            pltpu.SemaphoreType.DMA((4, RING - 1)),
+            pltpu.SemaphoreType.DMA((SHARDS,)),
+            pltpu.SemaphoreType.DMA((SHARDS,)),
+            pltpu.SemaphoreType.DMA((2, RING - 1)),
+            pltpu.SemaphoreType.DMA((2, RING - 1)),
             pltpu.SemaphoreType.DMA((2, 4, 15)),
             pltpu.SemaphoreType.DMA((2, 4, 15)),
         ],
@@ -590,7 +591,7 @@
     )(*args)
 
 
-TURN = 256
+TURN = 512
 
 
 def finish_kernel(
@@ -637,8 +638,8 @@
         small_out[...] = mine[0:1, 0:SEG]
         small_one_out[...] = mine[1:2, 0:SEG]
         small_two_out[...] = mine[2:3, 0:SEG]
-        small_weights_out[...] = small[0:1, 0:SMALL].astype(jnp.bfloat16)
-        small_average_out[...] = small[3:4, 0:SMALL]
+        small_weights_out[...] = small[0, 0:SMALL].astype(jnp.bfloat16)
+        small_average_out[...] = small[3, 0:SMALL]
 
 
 def finish(codes, smooth, master, one, two, small, mine):
@@ -654,7 +655,7 @@
         finish_kernel,
         grid=(pl.cdiv(COLS, TURN),),
         in_specs=[vmem] * 7,
-        out_specs=[turned, turned] + [whole(MINE, ALL_COLS)] * 3 + [whole(1, SEG)] * 3 + [whole(1, SMALL)] * 2,
+        out_specs=[turned, turned] + [whole(MINE, ALL_COLS)] * 3 + [whole(1, SEG)] * 3 + [whole(SMALL)] * 2,
         out_shape=(
             jax.ShapeDtypeStruct((COLS, SHARDS * ROWS), bf16),
             jax.ShapeDtypeStruct((COLS, SHARDS * ROWS), f32),
@@ -664,8 +665,8 @@
             few,
             few,
             few,
-            jax.ShapeDtypeStruct((1, SMALL), bf16),
-            jax.ShapeDtypeStruct((1, SMALL), f32),
+            jax.ShapeDtypeStruct((SMALL,), bf16),
+            jax.ShapeDtypeStruct((SMALL,), f32),
         ),
         compiler_params=pltpu.CompilerParams(vmem_limit_bytes=32 * 1024 * 1024),
         name="finish",
@@ -711,9 +712,9 @@
         small_new_one,
         small_new_two,
         weights.T,
-        small_weights.reshape(SMALL),
+        small_weights,
         averages.T,
-        small_averages.reshape(SMALL),
+        small_averages,
     )
 
 

time: 96.7 us -> 93.1 us (0.963)
  Pallas kernels: 92.6 us -> 90.9 us
  other arithmetic: 1.18 us -> 0 us
    pallas_call x2 -> x0, other arithmetic: 1.18 us -> none  [finish(): pl.pallas_call(finish_kernel, grid=(pl.cdiv(COLS, TURN),), in_specs=[vmem...]
    pallas_call x1, Pallas kernels: 8.1 us -> 6.97 us  [finish(): pl.pallas_call(finish_kernel, grid=(pl.cdiv(COLS, TURN),), in_specs=[vmem...]
where the time goes in v4:
time: 93.1 us; the launch traced here: 92.8 us
  Pallas kernels  90.9 us (98%)
  between operations  1.95 us (2%)
    pallas_call x1, Pallas kernels, communicate(): pl.pallas_call(step_kernel, out_shape=(*[pltpu.VMEM((MINE, ALL_COLS), f32...  83.9 us
    pallas_call x1, Pallas kernels, finish(): pl.pallas_call(finish_kernel, grid=(pl.cdiv(COLS, TURN),), in_specs=[vmem...  6.97 us

profile of v4, /device:TPU:1, one launch (start us, length us, event | category | flops | bytes accessed | tf_op | source)
XLA Modules:
  0.0 92.8 jit_solution(6089885621827734966)
XLA Ops:
  1.9 83.9 %step.2 = (f32[7,16640]{1,0:T(8,128)S(1)}, f32[7,16640]{1,0:T(8,128)S(1)}, f32[7,16640]{1,0:T(8,128)S(1)}, f32[8,384]{1,0:T(8,128)S(1)}, f32[8,128]{1,0:T(8,128)...) custom-call(s32[1]{0:T(128)S(6)} %copy.22.counts, s32[1]{0:T(128)S(6)} %copy.23.step, ...), custom_call_target="tpu_custom_call" | custom-call | tf_op jit(solution)/shard_map/step/pallas_call | solution.py:539
  85.9 7.0 %finish.1 = (bf16[2080,896]{1,0:T(8,128)(2,1)}, f32[2080,896]{1,0:T(8,128)}, f32[7,16640]{1,0:T(8,128)}, f32[7,16640]{1,0:T(8,128)}, f32[7,16640]{1,0:T(8,128)},...) custom-call(s16[16,56,2080]{2,1,0:T(8,128)(2,1)S(1)} %get-tuple-element.27.code, ...), custom_call_target="tpu_custom_call" | custom-call | tf_op jit(solution)/shard_map/finish/pallas_call | solution.py:654

commit v5 on v4

--- a/solution.py
+++ b/solution.py
@@ -162,6 +162,12 @@
     def shard_of(axis, p, k):
         return p * RING + k if axis == 0 else k * RING + p
 
+    barrier = pltpu.get_barrier_semaphore()
+    for d in range(1, SHARDS):
+        pl.semaphore_signal(barrier, inc=1, device_id=(wrap(s, d, SHARDS), t), device_id_type=MESH)
+    for d in range(1, TENSORS):
+        pl.semaphore_signal(barrier, inc=1, device_id=(s, wrap(t, d, TENSORS)), device_id_type=MESH)
+
     loads = [(average_hbm, pa)]
     for first, width in PARTS:
         cut = (slice(None), pl.ds(first, width))
@@ -179,13 +185,6 @@
     small_in[...] = exact_dot(small_state[...], place(s, (128, LANES), 0))
     micro = small_grads[...].astype(jnp.float32)
     small_in[0:1, pl.ds(0, SMALL)] = valid_one * micro[0:1] + valid_two * micro[1:2]
-
-    barrier = pltpu.get_barrier_semaphore()
-    for d in range(1, SHARDS):
-        pl.semaphore_signal(barrier, inc=1, device_id=(wrap(s, d, SHARDS), t), device_id_type=MESH)
-    for d in range(1, TENSORS):
-        pl.semaphore_signal(barrier, inc=1, device_id=(s, wrap(t, d, TENSORS)), device_id_type=MESH)
-    pl.semaphore_wait(barrier, SHARDS - 1 + TENSORS - 1)
 
     pending = []
 
@@ -225,9 +224,7 @@
         for j in range(4):
             achunk_send[4 * h + j] = encode(codes[:, COLS * j : COLS * (j + 1)], AVERAGE_MAX)
     achunk_recv[t] = achunk_send[t]
-    achunk_copies = exchange(3, achunk_send, achunk_recv)
-
-    small_copies = ring_share(0, 0, small_in, small_y)
+
 
     def turn(q, tile):
         first, width = PARTS[q]
@@ -348,6 +345,8 @@
                 return carry
 
             lax.fori_loop(0, RING, fill, 0)
+            if slot == 0 and q == 0:
+                pl.semaphore_wait(barrier, SHARDS - 1 + TENSORS - 1)
             to = wrap(p, -sign, RING) if slot == 0 else dest
             early[q][slot] = send(
                 big_send[q].at[slot],
@@ -356,6 +355,9 @@
                 rs_recv_sem.at[q, slot],
                 ring_device(axis, to),
             )
+            if slot == 0 and q == 1:
+                achunk_copies = exchange(3, achunk_send, achunk_recv)
+                small_copies = ring_share(0, 0, small_in, small_y)
     relayed = [[None] * RING for _ in range(4)]
     for q in range(4):
         early[q][0].wait_recv()

time: 93.1 us -> 92 us (0.988)
  Pallas kernels: 90.9 us -> 89.9 us
    pallas_call x1, Pallas kernels: 83.9 us -> 83 us  [communicate(): pl.pallas_call(step_kernel, out_shape=(*[pltpu.VMEM((MINE, ALL_COLS), f32...]
where the time goes in v5:
time: 92 us; the launch traced here: 91.9 us
  Pallas kernels  89.9 us (98%)
  between operations  1.95 us (2%)
    pallas_call x1, Pallas kernels, communicate(): pl.pallas_call(step_kernel, out_shape=(*[pltpu.VMEM((MINE, ALL_COLS), f32...  83 us
    pallas_call x1, Pallas kernels, finish(): pl.pallas_call(finish_kernel, grid=(pl.cdiv(COLS, TURN),), in_specs=[vmem...  6.97 us

profile of v5, /device:TPU:1, one launch (start us, length us, event | category | flops | bytes accessed | tf_op | source)
XLA Modules:
  0.0 91.9 jit_solution(16423125777108865580)
XLA Ops:
  1.9 83.0 %step.2 = (f32[7,16640]{1,0:T(8,128)S(1)}, f32[7,16640]{1,0:T(8,128)S(1)}, f32[7,16640]{1,0:T(8,128)S(1)}, f32[8,384]{1,0:T(8,128)S(1)}, f32[8,128]{1,0:T(8,128)...) custom-call(s32[1]{0:T(128)S(6)} %copy.22.counts, s32[1]{0:T(128)S(6)} %copy.23.step, ...), custom_call_target="tpu_custom_call" | custom-call | tf_op jit(solution)/shard_map/step/pallas_call | solution.py:541
  84.9 7.0 %finish.1 = (bf16[2080,896]{1,0:T(8,128)(2,1)}, f32[2080,896]{1,0:T(8,128)}, f32[7,16640]{1,0:T(8,128)}, f32[7,16640]{1,0:T(8,128)}, f32[7,16640]{1,0:T(8,128)},...) custom-call(s16[16,56,2080]{2,1,0:T(8,128)(2,1)S(1)} %get-tuple-element.27.code, ...), custom_call_target="tpu_custom_call" | custom-call | tf_op jit(solution)/shard_map/finish/pallas_call | solution.py:656

commit v6 on v5

--- a/solution.py
+++ b/solution.py
@@ -325,7 +325,7 @@
     early = [[None] * 2 for _ in range(4)]
     far = lax.min(lax.div(7 * wrap(pos[0], 2, RING), 4), 4)
     for slot in range(2):
-        for q in range(4):
+        for q in (0, 2, 1, 3):
             axis, sign = axes[q][0], signs[q]
             p = pos[axis]
             dest = wrap(p, 2, RING) if slot == 0 else wrap(p, sign, RING)
@@ -355,7 +355,7 @@
                 rs_recv_sem.at[q, slot],
                 ring_device(axis, to),
             )
-            if slot == 0 and q == 1:
+            if slot == 0 and q == 2:
                 achunk_copies = exchange(3, achunk_send, achunk_recv)
                 small_copies = ring_share(0, 0, small_in, small_y)
     relayed = [[None] * RING for _ in range(4)]
@@ -479,6 +479,8 @@
         load.wait()
     for copy in chunk_copies:
         copy.wait_recv()
+    for q in range(4):
+        gather_third(1, q)
     for h in range(2):
         cols = pl.ds(half * h, half)
         summed = jnp.concatenate([decode(chunk_recv[4 * h + j], 16 * SUM_MAX) for j in range(4)], axis=1)
@@ -490,8 +492,6 @@
             wchunk_send[4 * h + j] = encode_weight(new[:, COLS * j : COLS * (j + 1)])
     wchunk_recv[t] = wchunk_send[t]
     wchunk_copies = exchange(2, wchunk_send, wchunk_recv)
-    for q in range(4):
-        gather_third(1, q)
 
     new, one, two = adam(
         small_all[1:2], small_all[2:3], small_all[3:4], small_sum * factor, bias_one, bias_two, 0.0

time: 92 us -> 92 us (level)
  no operation moved by 1% of the time
where the time goes in v6:
time: 92 us; the launch traced here: 91.8 us
  Pallas kernels  89.9 us (98%)
  between operations  1.95 us (2%)
    pallas_call x1, Pallas kernels, communicate(): pl.pallas_call(step_kernel, out_shape=(*[pltpu.VMEM((MINE, ALL_COLS), f32...  82.9 us
    pallas_call x1, Pallas kernels, finish(): pl.pallas_call(finish_kernel, grid=(pl.cdiv(COLS, TURN),), in_specs=[vmem...  6.97 us

profile of v6, /device:TPU:1, one launch (start us, length us, event | category | flops | bytes accessed | tf_op | source)
XLA Modules:
  0.0 91.8 jit_solution(16798333834156696760)
XLA Ops:
  1.9 82.9 %step.2 = (f32[7,16640]{1,0:T(8,128)S(1)}, f32[7,16640]{1,0:T(8,128)S(1)}, f32[7,16640]{1,0:T(8,128)S(1)}, f32[8,384]{1,0:T(8,128)S(1)}, f32[8,128]{1,0:T(8,128)...) custom-call(s32[1]{0:T(128)S(6)} %copy.22.counts, s32[1]{0:T(128)S(6)} %copy.23.step, ...), custom_call_target="tpu_custom_call" | custom-call | tf_op jit(solution)/shard_map/step/pallas_call | solution.py:541
  84.8 7.0 %finish.1 = (bf16[2080,896]{1,0:T(8,128)(2,1)}, f32[2080,896]{1,0:T(8,128)}, f32[7,16640]{1,0:T(8,128)}, f32[7,16640]{1,0:T(8,128)}, f32[7,16640]{1,0:T(8,128)},...) custom-call(s16[16,56,2080]{2,1,0:T(8,128)(2,1)S(1)} %get-tuple-element.27.code, ...), custom_call_target="tpu_custom_call" | custom-call | tf_op jit(solution)/shard_map/finish/pallas_call | solution.py:656
